TPU v7x, 128 devices: a whole 4x4x4 slice. The times are simulated.
128 devices in a mesh: req: 4 (over y), seq: 32 (over x, z, core).
Axes of the slice: x: 4, y: 4, z: 4, core: 2. Of those that a mesh axis runs over, the one named last changes fastest.
Arguments:
- tokens: bfloat16 [4, 4096, 2048], P('req', 'seq'), may hold values from -6 to 6
- lengths: int32 [4, 4], replicated, may hold values from 1 to 2048, as said below
- attn_gain: bfloat16 [2048], replicated, may hold values from 0.099609375 to 1.8984375
- w_query: bfloat16 [2048, 512], replicated, may hold values from -0.125 to 0.125
- w_key: bfloat16 [2048, 512], replicated, may hold values from -0.125 to 0.125
- w_value: bfloat16 [2048, 1024], replicated, may hold values from -0.125 to 0.125
- w_outgate: bfloat16 [2048, 1024], replicated, may hold values from -0.125 to 0.125
- gate_down: bfloat16 [2048, 16], replicated, may hold values from -1 to 1
- gate_up: bfloat16 [16, 512], replicated, may hold values from -2 to 2
- gate_bias: float32 [512], replicated, may hold values from -1 to 8
- conv_weight: bfloat16 [4, 2048], replicated, may hold values from -2 to 2
- head_gain: bfloat16 [512], replicated, may hold values from 0.099609375 to 1.8984375
- w_out: bfloat16 [1024, 2048], replicated, may hold values from -0.1875 to 0.1875
- forward_norm_scale: bfloat16 [2048], replicated, may hold values from 0.099609375 to 1.8984375
- w_gate: bfloat16 [2048, 2816], P('seq', 'req'), may hold values from -0.125 to 0.125
- w_up: bfloat16 [2048, 2816], P('seq', 'req'), may hold values from -0.125 to 0.125
- down_weight: bfloat16 [2048, 2816], P('seq', 'req'), may hold values from -0.109375 to 0.109375
Outputs:
- output: bfloat16 [4, 4096, 2048], P('req', 'seq')
Inputs may be any that keep to these rules, and one draw needn't show every extreme that they name: Row g lists the prompt lengths of group g's 4 requests, packed in slot order from position 0 of the group; every row holds one length equal to 2048; rows 2i and 2i + 1 together sum to 6144, so all rows sum to 12288; each row sums to between 2052 and 4092.
All inputs are finite; a program needn't handle non-finite values.
Results may differ from a plain program's by a relative error of at most 0.008.
Values may be sent and summed in bfloat16 or wider, within the bound.
A program may use at most 128 MiB of HBM per device.

v0:
```python
import jax
import jax.numpy as jnp
from jax import lax
from jax.sharding import PartitionSpec as P

HEADS = 2
SPAN = 64


EPSILON = 1e-05
NORMALIZER = 16.0
MAXIMUM_ACCURACY = lax.Precision.HIGHEST


def prefix_2(shard, axis, combine, identity):
    size, mine = (lax.axis_size(axis), lax.axis_index(axis))
    everything = jax.tree.map(lambda part: lax.all_gather(part, axis), shard)
    start = jax.tree.map(
        lambda part, zero: jnp.broadcast_to(jnp.asarray(zero, part.dtype), part.shape),
        shard,
        identity,
    )

    def lap(k, before):
        reached = k < mine
        new = combine(before, jax.tree.map(lambda part: part[k], everything))
        return jax.tree.map(lambda a, b: jnp.where(reached, a, b), new, before)

    return lax.fori_loop(0, size, lap, start)


def from_behind(value, axis, steps):
    count = lax.axis_size(axis)
    initial, last = (max(0, -steps), min(count, count - steps))
    return lax.ppermute(value, axis, [(source, source + steps) for source in range(initial, last)])


def rms_scale(values, gain):
    mean_square = jnp.mean(values * values, axis=-1, keepdims=True)
    return values * lax.rsqrt(mean_square + EPSILON) * gain


def segment_ids(positions, bounds):
    return jnp.sum((positions[:, None] >= bounds[None, :]).astype(jnp.int32), axis=1)


def pick_group(table, indices):
    match = indices[:, None] == jnp.arange(table.shape[0], dtype=jnp.int32)[None, :]
    return jnp.sum(jnp.where(match, table[None, :], 0), axis=1)


def short_conv(extended, segment_ext, conv_weight, count):
    taps = conv_weight.shape[0]
    own_segment = segment_ext[taps - 1 :]
    total = jnp.zeros((count, extended.shape[1]), jnp.float32)
    for tap_index in range(taps):
        first = taps - 1 - tap_index
        shifted = extended[first : first + count].astype(jnp.float32)
        same = (segment_ext[first : first + count] == own_segment).astype(jnp.float32)
        total = total + conv_weight[tap_index].astype(jnp.float32) * shifted * same[:, None]
    return total


def span_cumulative(log_decay):
    span_len, head_count, key_width = log_decay.shape
    lower = jnp.tril(jnp.ones((span_len, span_len), jnp.float32))
    flat = jnp.dot(
        lower, log_decay.reshape(span_len, head_count * key_width), precision=MAXIMUM_ACCURACY
    )
    return flat.reshape(span_len, head_count, key_width)


def state_update(
    recurrent_state, cumulative, keys_float, value_rows_wide, segment_span, clean_last
):
    tail = cumulative[-1]
    keep = (segment_span == segment_span[-1]).astype(jnp.float32)
    weighted_values = keys_float * jnp.exp(tail[None] - cumulative) * keep[:, None, None]
    state_increment = jnp.einsum(
        "ugl,ugi->gli", weighted_values, value_rows_wide, precision=MAXIMUM_ACCURACY
    )
    return recurrent_state * (jnp.exp(tail) * clean_last)[:, :, None] + state_increment


def span_state(recurrent_state, items):
    query, keys, values, log_decay, segment_span, segment_before = items
    cumulative = span_cumulative(log_decay)
    clean_last = (segment_span[-1] == segment_before).astype(jnp.float32)
    new_state = state_update(
        recurrent_state,
        cumulative,
        keys.astype(jnp.float32),
        values.astype(jnp.float32),
        segment_span,
        clean_last,
    )
    return (new_state, None)


def span_attend(recurrent_state, items):
    query, keys, values, log_decay, segment_span, segment_before = items
    cumulative = span_cumulative(log_decay)
    query_float = query.astype(jnp.float32)
    keys_float = keys.astype(jnp.float32)
    clean = (segment_span == segment_before).astype(jnp.float32)
    query_decayed_rows = query_float * jnp.exp(cumulative) * clean[:, None, None]
    carried_forward = jnp.einsum(
        "ynj,njc->ync", query_decayed_rows, recurrent_state, precision=MAXIMUM_ACCURACY
    )
    order = jnp.arange(segment_span.shape[0])
    allowed = (segment_span[:, None] == segment_span[None, :]) & (order[:, None] >= order[None, :])
    gap = jnp.where(allowed[:, :, None, None], cumulative[:, None] - cumulative[None, :], 0.0)
    scores = jnp.sum(query_float[:, None] * keys_float[None, :] * jnp.exp(gap), axis=-1)
    scores = scores * allowed[:, :, None].astype(jnp.float32)
    inner = jnp.einsum(
        "tsh,shv->thv", scores.astype(jnp.bfloat16), values, preferred_element_type=jnp.float32
    )
    new_state = state_update(
        recurrent_state, cumulative, keys_float, values.astype(jnp.float32), segment_span, clean[-1]
    )
    return (new_state, (carried_forward + inner, cumulative))


def combine_states(earlier, later):
    return (earlier[0] * later[0], later[0][:, :, None] * earlier[1] + later[1])


def carry_in(decay_block, block_state):
    identity = (jnp.ones_like(decay_block), jnp.zeros_like(block_state))
    prefix = prefix_2((decay_block, block_state), "seq", combine_states, identity)
    return prefix[1]


def swiglu_rows(resident, forward_norm_scale, w_gate, w_up, down_weight):
    normed = rms_scale(resident.astype(jnp.float32), forward_norm_scale.astype(jnp.float32)).astype(
        jnp.bfloat16
    )
    every_row = lax.all_gather(normed, "req", axis=0, tiled=True)
    gate_full, up_full, down_full = (
        lax.all_gather(w_gate, "seq", axis=0, tiled=True),
        lax.all_gather(w_up, "seq", axis=0, tiled=True),
        lax.all_gather(down_weight, "seq", axis=0, tiled=True),
    )
    gate = jnp.dot(every_row, gate_full, preferred_element_type=jnp.float32)
    upward = jnp.dot(every_row, up_full, preferred_element_type=jnp.float32)
    hidden = (jax.nn.silu(gate) * upward).astype(jnp.bfloat16)
    summed = lax.psum_scatter(
        lax.dot_general(
            hidden, down_full, (((1,), (1,)), ((), ())), preferred_element_type=jnp.float32
        ),
        "req",
        scatter_dimension=0,
        tiled=True,
    )
    return summed.astype(jnp.bfloat16)


def shards(
    tokens,
    lengths,
    attn_gain,
    w_query,
    w_key,
    w_value,
    w_outgate,
    gate_down,
    gate_up,
    gate_bias,
    conv_weight,
    head_gain,
    w_out,
    forward_norm_scale,
    w_gate,
    w_up,
    down_weight,
):
    seq_count = lax.axis_size("seq")
    req_count = lax.axis_size("req")
    group_index = lax.axis_index("req")
    slice_index = lax.axis_index("seq")
    inputs = tokens[0]
    block_rows = inputs.shape[0]
    request_slots = lengths.shape[1]
    bounds_all = jnp.cumsum(lengths, axis=1)
    totals = bounds_all[:, -1]
    offsets = jnp.cumsum(totals) - totals
    group_row = jnp.arange(lengths.shape[0], dtype=jnp.int32) == group_index
    bounds = jnp.sum(jnp.where(group_row[:, None], bounds_all, 0), axis=0)
    start_pos = slice_index * block_rows
    positions = start_pos + jnp.arange(block_rows, dtype=jnp.int32)
    segment = segment_ids(positions, bounds)
    valid = segment < request_slots
    normed = rms_scale(inputs.astype(jnp.float32), attn_gain.astype(jnp.float32)).astype(
        jnp.bfloat16
    )
    projected = jnp.concatenate(
        [
            jnp.dot(normed, w_query, preferred_element_type=jnp.float32),
            jnp.dot(normed, w_key, preferred_element_type=jnp.float32),
            jnp.dot(normed, w_value, preferred_element_type=jnp.float32),
        ],
        axis=1,
    ).astype(jnp.bfloat16)
    outgate = jnp.dot(normed, w_outgate, preferred_element_type=jnp.float32)
    latent = jnp.dot(normed, gate_down, preferred_element_type=jnp.float32)
    logits = jnp.dot(latent, gate_up.astype(jnp.float32), precision=MAXIMUM_ACCURACY) + gate_bias
    log_decay = jax.nn.log_sigmoid(logits) / NORMALIZER
    taps = conv_weight.shape[0]
    edge_rows = projected[block_rows - (taps - 1) :]
    previous = from_behind(edge_rows, "seq", 1)
    extended = jnp.concatenate([previous, projected], axis=0)
    segment_ext = segment_ids(
        start_pos - (taps - 1) + jnp.arange(block_rows + taps - 1, dtype=jnp.int32), bounds
    )
    convolved = jax.nn.silu(short_conv(extended, segment_ext, conv_weight, block_rows)).astype(
        jnp.bfloat16
    )
    key_total = w_query.shape[1]
    value_total = w_value.shape[1]
    key_width = key_total // HEADS
    value_width = value_total // HEADS
    span_count = block_rows // SPAN
    query = convolved[:, :key_total].reshape(span_count, SPAN, HEADS, key_width)
    keys = convolved[:, key_total : 2 * key_total].reshape(span_count, SPAN, HEADS, key_width)
    values = convolved[:, 2 * key_total :].reshape(span_count, SPAN, HEADS, value_width)
    decay_spans = log_decay.reshape(span_count, SPAN, HEADS, key_width)
    segment_spans = segment.reshape(span_count, SPAN)
    segment_before = segment_ids(
        start_pos - 1 + SPAN * jnp.arange(span_count, dtype=jnp.int32), bounds
    )
    items = (query, keys, values, decay_spans, segment_spans, segment_before)
    block_clean = (segment[-1] == segment_before[0]).astype(jnp.float32)
    decay_block = jnp.exp(jnp.sum(log_decay, axis=0)).reshape(HEADS, key_width) * block_clean
    zero_state = jnp.zeros((HEADS, key_width, value_width), jnp.float32)
    block_state, unused = lax.scan(span_state, zero_state, items)
    incoming = carry_in(decay_block, block_state)
    final_state, (attended, cumulative) = lax.scan(span_attend, incoming, items)
    attended = attended.reshape(block_rows, HEADS, value_width)
    gated = rms_scale(attended, head_gain.astype(jnp.float32)).reshape(
        block_rows, value_total
    ) * jax.nn.silu(outgate)
    resident = (
        jnp.dot(gated.astype(jnp.bfloat16), w_out, preferred_element_type=jnp.float32)
        + inputs.astype(jnp.float32)
    ).astype(jnp.bfloat16)
    dev_count = req_count * seq_count
    own_index = group_index * seq_count + slice_index
    parallel_width = block_rows // dev_count
    capacity = 3 * block_rows // 4
    own_total = jnp.sum(jnp.where(group_row, totals, 0))
    own_offset = jnp.sum(jnp.where(group_row, offsets, 0))
    own_count = jnp.clip(own_total - start_pos, 0, block_rows)
    own_phase = (own_offset + start_pos) % dev_count
    target_slots = jnp.arange(dev_count, dtype=jnp.int32)[:, None]
    lanes = jnp.arange(parallel_width, dtype=jnp.int32)[None, :]
    source_rows = (target_slots - own_phase) % dev_count + lanes * dev_count
    outgoing = jnp.take(resident, source_rows.reshape(-1), axis=0).reshape(
        dev_count, parallel_width, -1
    )
    outgoing = jnp.where((source_rows < own_count)[:, :, None], outgoing, 0)
    arrived = lax.all_to_all(
        outgoing, ("req", "seq"), split_axis=0, concat_axis=0, tiled=True
    ).reshape(dev_count * parallel_width, -1)
    ranks = jnp.arange(capacity, dtype=jnp.int32) * dev_count + own_index
    owner = jnp.sum((ranks[:, None] >= offsets[None, :]).astype(jnp.int32), axis=1) - 1
    owner_offset = pick_group(offsets, owner)
    within = ranks - owner_offset
    owner_slice = within // block_rows
    owner_phase = (owner_offset + owner_slice * block_rows) % dev_count
    owner_lane = (owner_phase + within % block_rows) // dev_count - (
        own_index < owner_phase
    ).astype(jnp.int32)
    gathered = jnp.take(
        arrived, (owner * seq_count + owner_slice) * parallel_width + owner_lane, axis=0
    )
    processed = swiglu_rows(gathered, forward_norm_scale, w_gate, w_up, down_weight)
    senders = jnp.arange(dev_count, dtype=jnp.int32)
    sender_group = senders // seq_count
    sender_slice = senders % seq_count
    sender_base = pick_group(offsets, sender_group) + sender_slice * block_rows
    sender_phase = sender_base % dev_count
    sender_rows = (own_index - sender_phase[:, None]) % dev_count + lanes * dev_count
    sender_count = jnp.clip(
        pick_group(totals, sender_group) - sender_slice * block_rows, 0, block_rows
    )
    home_slot = jnp.clip((sender_base[:, None] + sender_rows) // dev_count, 0, capacity - 1)
    returning = jnp.take(processed, home_slot.reshape(-1), axis=0).reshape(
        dev_count, parallel_width, -1
    )
    returning = jnp.where((sender_rows < sender_count[:, None])[:, :, None], returning, 0)
    returned = lax.all_to_all(
        returning, ("req", "seq"), split_axis=0, concat_axis=0, tiled=True
    ).reshape(dev_count * parallel_width, -1)
    device_local_rows = jnp.arange(block_rows, dtype=jnp.int32)
    target_of = (own_phase + device_local_rows) % dev_count
    lane_of = (own_phase + device_local_rows) // dev_count - (target_of < own_phase).astype(
        jnp.int32
    )
    mlp_own = jnp.take(
        returned,
        jnp.clip(target_of * parallel_width + lane_of, 0, dev_count * parallel_width - 1),
        axis=0,
    )
    output = jnp.where(
        valid[:, None], resident.astype(jnp.float32) + mlp_own.astype(jnp.float32), 0.0
    ).astype(jnp.bfloat16)
    return output[None]


def solution(mesh):
    return jax.shard_map(
        shards,
        mesh=mesh,
        in_specs=(
            P("req", "seq", None),
            P(),
            P(),
            P(),
            P(),
            P(),
            P(),
            P(),
            P(),
            P(),
            P(),
            P(),
            P(),
            P(),
            P("seq", "req"),
            P("seq", "req"),
            P("seq", "req"),
        ),
        out_specs=P("req", "seq", None),
        check_vma=False,
    )
```

profile of v0, /device:TPU:1, one launch (start us, length us, event | category | flops | bytes accessed | tf_op | source)
XLA Modules:
  0.0 449.4 jit_solution(5662476398953703670)
XLA Ops:
  8.6 3.3 convolution_convert_fusion
  13.1 4.9 %collective-permute-start = (bf16[3,2048]{1,0:T(4,128)(2,1)S(1)}, bf16[3,2048]{1,0:T(4,128)(2,1)S(1)}, u32[]{:S(2)}, u32[]{:S(2)}) collective-permute-start(bf16[3,2048]{1,0:T(4,128)(2,1)S(1)} %slice.105), channel_id=1, source_target_pairs={{0,1},{1,2},{2,3},{3,4},{4,5},{5,6},{6,7},{7,8},{8,9},{9,10},{10,1... | collective-permute-start | bytes 36872 | tf_op jit(solution)/shard_map/ppermute | solution.py:35
  21.2 9.2 %while.38 = (s32[]{:T(128)}, f32[2,256,512]{2,1,0:T(8,128)S(1)}, f32[2,64,2,256]{3,2,1,0:T(2,128)S(1)}, s32[2,64]{1,0:T(2,128)S(1)}, s32[2]{0:T(128)S(1)}, /*ind...) while((s32[]{:T(128)}, f32[2,256,512]{2,1,0:T(8,128)S(1)}, ...), condition=%wide.region_8.9_spmd.clone, body=%wide.region_7.8_spmd.clone.sunk | while | flops 227418752 | bytes 3230365 | solution.py:235
  35.1 26.4 %all_gather.22 = f32[32,2,256]{2,1,0:T(2,128)S(1)} all-gather(f32[1,2,256]{2,1,0:T(2,128)S(1)} %mul.395), channel_id=1, replica_groups=mesh['req'=4,'seq'=32] {'seq'}, dimensions={0}, use_global_device_ids=true | all-gather | bytes 67584 | tf_op jit(solution)/shard_map/all_gather | solution.py:17
  62.5 84.9 %all-gather.15.cloned.1.call-done = f32[64,256,512]{2,1,0:T(8,128)} async-done(((f32[2,256,512]{2,1,0:T(8,128)}), f32[64,256,512]{2,1,0:T(8,128)}) %all-gather.15.cloned.1.call-update) | async-done | bytes 33554448 | tf_op jit(solution)/shard_map/all_gather | solution.py:17
  147.4 49.0 %while.39 = (s32[]{:T(128)}, f32[2,256,512]{2,1,0:T(8,128)S(1)}, s32[]{:T(128)}, f32[32,2,256]{2,1,0:T(2,128)S(1)}, f32[32,2,256,512]{3,2,1,0:T(8,128)}, /*index=5*/s32[]{:T(128)}, s32[]{:T(128)}) while((s32[]{:T(128)}, f32[2,256,512]{2,1,0:T(8,128)S(1)}, s32[]{:T(128)}, f32[32,2,256]{2,1,0:T(2,128)S(1)}, ...), condition=%wide.region_10.11_spmd.clone, body=%wide.region_9.10_spmd.clone.sunk | while | flops 1048580 | bytes 3151977 | solution.py:29
  149.0 1.5 fusion.165
  150.5 1.5 fusion.165
  152.0 1.5 fusion.165
  153.6 1.5 fusion.165
  155.1 1.5 fusion.165
  156.6 1.5 fusion.165
  158.1 1.5 fusion.165
  159.7 1.5 fusion.165
  161.2 1.5 fusion.165
  162.7 1.5 fusion.165
  164.3 1.5 fusion.165
  165.8 1.5 fusion.165
  167.3 1.5 fusion.165
  168.9 1.5 fusion.165
  170.4 1.5 fusion.165
  171.9 1.5 fusion.165
  173.4 1.5 fusion.165
  176.5 1.5 fusion.165
  178.0 1.5 fusion.165
  181.1 1.5 fusion.165
  182.7 1.5 fusion.165
  184.2 1.5 fusion.165
  188.8 1.5 fusion.165
  190.4 1.5 fusion.165
  191.9 1.5 fusion.165
  193.4 1.5 fusion.165
  196.5 19.7 %while.37 = (s32[]{:T(128)}, f32[2,256,512]{2,1,0:T(8,128)S(1)}, f32[2,64,2,512]{3,1,2,0:T(8,128)S(1)}, f32[2,64,2,256]{3,2,1,0:T(2,128)S(1)}, s32[2,64]{1,0:T(2...) while((s32[]{:T(128)}, f32[2,256,512]{2,1,0:T(8,128)S(1)}, ...), condition=%wide.region_13.14_spmd, body=%wide.region_11.13_spmd.sunk | while | flops 447611648 | bytes 7385501 | solution.py:237
  198.6 3.0 multiply_reduce_fusion.3
  208.4 3.0 multiply_reduce_fusion.3
  217.2 4.9 %fusion.53 = bf16[128,2048]{1,0:T(8,128)(2,1)S(1)} fusion(bf16[1024,2048]{1,0:T(8,128)(2,1)} %param.37, bf16[1,128,2048]{2,1,0:T(8,128)(2,1)S(1)} %copy-done.3, f32[128,1024]{1,0:T(8,128)S(1)} %bitcast.254, f32[128,1024]{1,0:T(8,128)S(1)} %bitcast.253, f32[1024]{0:T(1024)S(1)} %bitcast.261, bf16[2048,1024]{1,0:T(8,128)(2,1)} %param.31, ...), kind=kOutput, calls=%fused_computation.82 | convolution fusion | flops 1076625408 | bytes 10498560 | tf_op jit(solution)/shard_map/dot_general | solution.py:243
  226.0 7.1 %all-to-all-start = ((bf16[128,2,1024]{2,1,0:T(2,128)(2,1)}), bf16[128,2,1024]{2,1,0:T(2,128)(2,1)S(1)}, u32[]{:S(2)}, u32[]{:S(2)}) async-start(bf16[128,2,1024]{2,1,0:T(2,128)(2,1)} %reshape.936), calls=%async_computation | async-start | bytes 1048576 | tf_op jit(solution)/shard_map/all_to_all | solution.py:261
  233.3 13.4 %all-to-all-done = bf16[128,2,1024]{2,1,0:T(2,128)(2,1)S(1)} async-done(((bf16[128,2,1024]{2,1,0:T(2,128)(2,1)}), bf16[128,2,1024]{2,1,0:T(2,128)(2,1)S(1)}, u32[]{:S(2)}, u32[]{:S(2)}) %all-to-all-start) | async-done | bytes 524320 | tf_op jit(solution)/shard_map/all_to_all | solution.py:261
  251.3 21.3 %all-gather.7.cloned.1.call-done = bf16[384,2048]{1,0:T(8,128)(2,1)} async-done(((bf16[96,2048]{1,0:T(8,128)(2,1)}), bf16[384,2048]{1,0:T(8,128)(2,1)}) %all-gather.7.cloned.1.call-update) | async-done | bytes 1572880 | tf_op jit(solution)/shard_map/all_gather | solution.py:138
  272.6 5.2 %fusion.111 = f32[384,704]{0,1:T(8,128)} fusion(bf16[384,2048]{1,0:T(8,128)(2,1)} %all-gather.7.cloned.1.call-done, bf16[2048,704]{1,0:T(8,128)(2,1)} %all-gather.9.cloned.1.call-done), kind=kOutput, calls=%fused_computation.264 | convolution fusion | flops 1107296256 | bytes 5537792 | tf_op jit(solution)/shard_map/dot_general | solution.py:144
  277.7 42.4 %all-gather.11.cloned.1.call-done = bf16[2048,704]{1,0:T(8,128)(2,1)} async-done(((bf16[64,704]{1,0:T(8,128)(2,1)}), bf16[2048,704]{1,0:T(8,128)(2,1)}) %all-gather.11.cloned.1.call-update) | async-done | bytes 2883600 | tf_op jit(solution)/shard_map/all_gather | solution.py:141
  320.2 46.3 %all-gather.13.cloned.1.call-done = bf16[2048,704]{1,0:T(8,128)(2,1)} async-done(((bf16[64,704]{1,0:T(8,128)(2,1)}), bf16[2048,704]{1,0:T(8,128)(2,1)}) %all-gather.13.cloned.1.call-update) | async-done | bytes 2883600 | tf_op jit(solution)/shard_map/all_gather | solution.py:142
  366.5 7.9 %fusion.62 = f32[384,2048]{1,0:T(8,128)} fusion(bf16[2048,704]{1,0:T(8,128)(2,1)} %all-gather.13.cloned.1.call-done, bf16[384,2048]{1,0:T(8,128)(2,1)S(1)} %copy-done.9, bf16[2048,704]{1,0:T(8,128)(2,1)} %all-gather.11.cloned.1.call-done, f32[384,704]{0,1:T(8,128)} %fusion.111), kind=kOutput, calls=%fused_computation.103 | convolution fusion | flops 2216214528 | bytes 11567104 | tf_op jit(solution)/shard_map/dot_general | solution.py:148
  374.7 37.1 %reduce-scatter.2.cloned.1.call-done = f32[96,2048]{1,0:T(8,128)} async-done(((f32[384,2048]{1,0:T(8,128)}), f32[96,2048]{1,0:T(8,128)}) %reduce-scatter.2.cloned.1.call-update) | async-done | bytes 786448 | tf_op jit(solution)/shard_map/reduce_scatter | solution.py:147
  416.2 8.0 %all-to-all-start.1 = ((bf16[128,2,1024]{2,1,0:T(2,128)(2,1)}), bf16[128,2,1024]{2,1,0:T(2,128)(2,1)S(1)}, u32[]{:S(2)}, u32[]{:S(2)}) async-start(bf16[128,2,1024]{2,1,0:T(2,128)(2,1)} %reshape.938), calls=%async_computation.2 | async-start | bytes 1048576 | tf_op jit(solution)/shard_map/all_to_all | solution.py:291
  424.3 13.5 %all-to-all-done.1 = bf16[128,2,1024]{2,1,0:T(2,128)(2,1)S(1)} async-done(((bf16[128,2,1024]{2,1,0:T(2,128)(2,1)}), bf16[128,2,1024]{2,1,0:T(2,128)(2,1)S(1)}, u32[]{:S(2)}, u32[]{:S(2)}) %all-to-all-start.1) | async-done | bytes 524320 | tf_op jit(solution)/shard_map/all_to_all | solution.py:291
  438.6 1.7 gather_fusion.3
  440.3 2.2 fusion.64
  (231 shorter events, 53.9 us)
Async XLA Ops:
  6.5 5.4 %copy-start = (bf16[2048,512]{1,0:T(8,128)(2,1)S(1)}, bf16[2048,512]{1,0:T(8,128)(2,1)}, u32[]{:S(2)}) copy-start(bf16[2048,512]{1,0:T(8,128)(2,1)} %param.29) | copy-start | bytes 6291460
  6.5 5.4 %copy-start.3 = (bf16[1,128,2048]{2,1,0:T(8,128)(2,1)S(1)}, bf16[1,128,2048]{2,1,0:T(8,128)(2,1)}, u32[]{:S(2)}) copy-start(bf16[1,128,2048]{2,1,0:T(8,128)(2,1)} %param.25) | copy-start | bytes 1572868
  6.5 140.9 %all-gather.15.cloned.1.call-start = ((), (), s32[]{:S(2)}) async-start(), calls=%async_computation.8 | async-start | bytes 34603008 | tf_op jit(solution)/shard_map/all_gather | solution.py:17
  8.6 3.8 copy-start.8
  11.9 6.1 %copy-start.6 = (s32[4,4]{1,0:T(4,128)S(1)}, s32[4,4]{1,0:T(4,128)}, u32[]{:S(2)}) copy-start(s32[4,4]{1,0:T(4,128)} %param.26) | copy-start | bytes 196
  11.9 6.6 %copy-start.4 = (bf16[4,2048]{1,0:T(4,128)(2,1)S(1)}, bf16[4,2048]{1,0:T(4,128)(2,1)}, u32[]{:S(2)}) copy-start(bf16[4,2048]{1,0:T(4,128)(2,1)} %param.35) | copy-start | bytes 49156
  11.9 6.7 %copy-start.10 = (bf16[2048,16]{0,1:T(8,128)(2,1)S(1)}, bf16[2048,16]{0,1:T(8,128)(2,1)}, u32[]{:S(2)}) copy-start(bf16[2048,16]{0,1:T(8,128)(2,1)} %param.32) | copy-start | bytes 196612
  12.5 6.5 %copy-start.11 = (bf16[16,512]{1,0:T(8,128)(2,1)S(1)}, bf16[16,512]{1,0:T(8,128)(2,1)}, u32[]{:S(2)}) copy-start(bf16[16,512]{1,0:T(8,128)(2,1)} %param.33) | copy-start | bytes 49156
  12.5 6.5 %copy-start.12 = (f32[512]{0:T(512)S(1)}, f32[512]{0:T(512)}, u32[]{:S(2)}) copy-start(f32[512]{0:T(512)} %param.34) | copy-start | bytes 6148
  13.1 6.8 %collective-permute-start = (bf16[3,2048]{1,0:T(4,128)(2,1)S(1)}, bf16[3,2048]{1,0:T(4,128)(2,1)S(1)}, u32[]{:S(2)}, u32[]{:S(2)}) collective-permute-start(bf16[3,2048]{1,0:T(4,128)(2,1)S(1)} %slice.105), channel_id=1, source_target_pairs={{0,1},{1,2},{2,3},{3,4},{4,5},{5,6},{6,7},{7,8},{8,9},{9,10},{10,1... | collective-permute-start | bytes 36872 | tf_op jit(solution)/shard_map/ppermute | solution.py:35
  21.2 40.4 %copy-start.7 = (bf16[512]{0:T(512)(128)(2,1)S(1)}, bf16[512]{0:T(512)(128)(2,1)}, u32[]{:S(2)}) copy-start(bf16[512]{0:T(512)(128)(2,1)} %param.36) | copy-start | bytes 3076
  21.2 41.3 %copy-start.5 = (bf16[2048]{0:T(1024)(128)(2,1)S(1)}, bf16[2048]{0:T(1024)(128)(2,1)}, u32[]{:S(2)}) copy-start(bf16[2048]{0:T(1024)(128)(2,1)} %param.38) | copy-start | bytes 12292
  30.4 1.0 copy-start.2
  31.5 219.8 %all-gather.9.cloned.1.call-start = ((), (), s32[]{:S(2)}) async-start(), calls=%async_computation.4 | async-start | bytes 3244032 | tf_op jit(solution)/shard_map/all_gather | solution.py:140
  226.0 20.7 %all-to-all-start = ((bf16[128,2,1024]{2,1,0:T(2,128)(2,1)}), bf16[128,2,1024]{2,1,0:T(2,128)(2,1)S(1)}, u32[]{:S(2)}, u32[]{:S(2)}) async-start(bf16[128,2,1024]{2,1,0:T(2,128)(2,1)} %reshape.936), calls=%async_computation | async-start | bytes 1048576 | tf_op jit(solution)/shard_map/all_to_all | solution.py:261
  233.2 39.4 %all-gather.7.cloned.1.call-start = ((), (), s32[]{:S(2)}) async-start(), calls=%async_computation.3 | async-start | bytes 1966080 | tf_op jit(solution)/shard_map/all_gather | solution.py:138
  249.8 70.3 %all-gather.11.cloned.1.call-start = ((), (), s32[]{:S(2)}) async-start(), calls=%async_computation.5 | async-start | bytes 3244032 | tf_op jit(solution)/shard_map/all_gather | solution.py:141
  250.4 116.1 %all-gather.13.cloned.1.call-start = ((), (), s32[]{:S(2)}) async-start(), calls=%async_computation.6 | async-start | bytes 3244032 | tf_op jit(solution)/shard_map/all_gather | solution.py:142
  251.0 160.7 %reduce-scatter.2.cloned.1.call-start = ((), (), s32[]{:S(2)}) async-start(), calls=%async_computation.7 | async-start | bytes 3932160 | tf_op jit(solution)/shard_map/reduce_scatter | solution.py:147
  272.6 93.9 %copy-start.9 = (bf16[384,2048]{1,0:T(8,128)(2,1)S(1)}, bf16[384,2048]{1,0:T(8,128)(2,1)}, u32[]{:S(2)}) copy-start(bf16[384,2048]{1,0:T(8,128)(2,1)} %all-gather.7.cloned.1.call-done) | copy-start | bytes 4718596
  416.2 21.6 %all-to-all-start.1 = ((bf16[128,2,1024]{2,1,0:T(2,128)(2,1)}), bf16[128,2,1024]{2,1,0:T(2,128)(2,1)S(1)}, u32[]{:S(2)}, u32[]{:S(2)}) async-start(bf16[128,2,1024]{2,1,0:T(2,128)(2,1)} %reshape.938), calls=%async_computation.2 | async-start | bytes 1048576 | tf_op jit(solution)/shard_map/all_to_all | solution.py:291
  438.6 4.0 copy-start.1
Sparse Core Ops, SparseCore 0:
  31.6 115.7 all-gather.14
  149.7 44.1 all-gather.8
  250.0 22.5 all-gather.6
  274.7 45.4 all-gather.10
  322.3 44.2 all-gather.12
  374.6 37.1 reduce-scatter.1
where the time goes:
time: 451 us; the launch traced here: 449 us
  waiting for transfers between devices  261 us (58%)
  other arithmetic  71.9 us (16%)
  matrix products  29.9 us (7%)
  blocking collectives  26.4 us (6%)
  starting transfers between devices  20.5 us (5%)
  local copies, waits for them, and re-layouts  19.7 us (4%)
  between operations  15.9 us (4%)
    all_gather x1, waiting for transfers between devices, prefix_2(): everything = jax.tree.map(lambda part: lax.all_gather(part, axis), shard)  84.9 us
    select_n x32, other arithmetic, lap(): return jax.tree.map(lambda a, b: jnp.where(reached, a, b), new, before)  47.7 us
    all_gather x1, waiting for transfers between devices, swiglu_rows(): lax.all_gather(down_weight, 'seq', axis=0, tiled=True)  46.3 us
    all_gather x1, waiting for transfers between devices, swiglu_rows(): lax.all_gather(w_up, 'seq', axis=0, tiled=True)  42.4 us
    reduce_scatter x1, waiting for transfers between devices, swiglu_rows(): lax.psum_scatter(lax.dot_general(hidden, down_full, (((1,), (1,)), ((), (...  37.1 us
    all_gather x1, blocking collectives, prefix_2(): everything = jax.tree.map(lambda part: lax.all_gather(part, axis), shard)  26.4 us
    all_gather x1, waiting for transfers between devices, swiglu_rows(): every_row = lax.all_gather(normed, 'req', axis=0, tiled=True)  21.3 us
    all_to_all x1, waiting for transfers between devices, shards(): lax.all_to_all(returning, ('req', 'seq'), split_axis=0, concat_axis=0, ti...  13.5 us
  transfers between devices with their start and end apart: 9, of which 7 were waited for; matrix products, arithmetic and copies ran while one was open for 20% of the time, Pallas kernels for 0%

commit v1 on v0

v1 whole, which is shorter than its diff:
```python
import functools

import jax
import jax.numpy as jnp
from jax import lax
from jax.experimental import pallas as pl
from jax.experimental.pallas import tpu as pltpu
from jax.sharding import PartitionSpec as P

HEADS = 2
EPSILON = 1e-05
NORMALIZER = 16.0
HIGHEST = lax.Precision.HIGHEST
MESH = pl.DeviceIdType.MESH

SIDE = 4
BLOCKS = SIDE**3
HALF = 384
ORDERS = (("x", "y", "z"), ("y", "z", "x"), ("z", "x", "y"))


def place():
    seq = lax.axis_index("seq")
    return {
        "x": seq // (2 * SIDE),
        "z": (seq // 2) % SIDE,
        "y": lax.axis_index("req"),
        "c": seq % 2,
    }


def device_at(at):
    return (at["y"], (at["x"] * SIDE + at["z"]) * 2 + at["c"])


def moved(at, axis, by):
    new = dict(at)
    new[axis] = (at[axis] + by + SIDE) % SIDE
    return new


def block_of(at):
    return at["y"] * (SIDE * SIDE) + at["x"] * SIDE + at["z"]


def gather_kernel(rows, *refs):
    shards, fulls = refs[:3], refs[3:6]
    local_sem, pair_send, pair_recv, send_sem, recv_sem = refs[6:]
    me = place()
    core = me["c"]
    sibling = dict(me, c=1 - core)
    barrier = pltpu.get_barrier_semaphore()
    partners = [moved(me, axis, by) for axis in "xyz" for by in (1, -1)] + [sibling]
    for partner in partners:
        pl.semaphore_signal(barrier, inc=1, device_id=device_at(partner), device_id_type=MESH)
    pl.semaphore_wait(barrier, len(partners))

    def slot(part, at):
        return fulls[part].at[pl.ds(pl.multiple_of(block_of(at) * 2 * rows, 128), 2 * rows), :]

    def half(part, at, source_core):
        first = pl.multiple_of((block_of(at) * 2 + source_core) * rows, 64)
        return fulls[part].at[pl.ds(first, rows), :]

    def columns(part, which):
        return shards[part].at[:, pl.ds(pl.multiple_of(which * HALF, 128), HALF)]

    locals_, pairs = [], []
    for part in range(3):
        pair = pltpu.make_async_remote_copy(
            src_ref=columns(part, 1 - core),
            dst_ref=half(part, me, core),
            send_sem=pair_send.at[part],
            recv_sem=pair_recv.at[part],
            device_id=device_at(sibling),
            device_id_type=MESH,
        )
        pair.start()
        pairs.append(pair)
        own = pltpu.make_async_copy(columns(part, core), half(part, me, core), local_sem.at[part])
        own.start()
        locals_.append(own)

    def send(part, at, axis, by):
        pltpu.make_async_remote_copy(
            src_ref=slot(part, at),
            dst_ref=slot(part, at),
            send_sem=send_sem.at[part],
            recv_sem=recv_sem.at[part, block_of(at)],
            device_id=device_at(moved(me, axis, by)),
            device_id_type=MESH,
        ).start()

    def arrive(part, at):
        pltpu.make_async_remote_copy(
            src_ref=slot(part, at),
            dst_ref=slot(part, at),
            send_sem=send_sem.at[part],
            recv_sem=recv_sem.at[part, block_of(at)],
            device_id=device_at(sibling),
            device_id_type=MESH,
        ).wait_recv()

    def both(part, at, axis):
        send(part, at, axis, 1)
        send(part, at, axis, -1)

    onward = 1 - 2 * core

    for part in range(3):
        locals_[part].wait()
        pairs[part].wait_recv()
        both(part, me, ORDERS[part][0])
    for part in range(3):
        both(part, me, ORDERS[part][1])
    for part in range(3):
        both(part, me, ORDERS[part][2])

    for kind, by in enumerate((-onward, onward, 2)):
        for part in range(3):
            first, second, third = ORDERS[part]
            at = dict(me)
            at[first] = (me[first] + by + SIDE) % SIDE
            arrive(part, at)
            if kind == 0:
                send(part, at, first, onward)
            both(part, at, second)
            both(part, at, third)

    for kind, by in enumerate((-onward, onward, 2)):
        def along_first(step, carry, kind=kind, by=by):
            for part in range(3):
                first, second, third = ORDERS[part]
                at = dict(me)
                at[first] = (me[first] + step) % SIDE
                at[second] = (me[second] + by + SIDE) % SIDE
                arrive(part, at)
                if kind == 0:
                    send(part, at, second, onward)
                both(part, at, third)
            return carry

        lax.fori_loop(0, SIDE, along_first, 0)

    for kind, by in enumerate((-onward, onward, 2)):
        def along_two(step, carry, kind=kind, by=by):
            for part in range(3):
                first, second, third = ORDERS[part]
                at = dict(me)
                at[first] = (me[first] + step % SIDE) % SIDE
                at[second] = (me[second] + step // SIDE) % SIDE
                at[third] = (me[third] + by + SIDE) % SIDE
                arrive(part, at)
                if kind == 0:
                    send(part, at, third, onward)
            return carry

        lax.fori_loop(0, SIDE * SIDE, along_two, 0)

    for part in range(3):
        pairs[part].wait_send()
        sent = fulls[part].at[pl.ds(0, (BLOCKS - 1) * 2 * rows), :]
        pltpu.make_async_remote_copy(
            src_ref=sent,
            dst_ref=sent,
            send_sem=send_sem.at[part],
            recv_sem=recv_sem.at[part, 0],
            device_id=device_at(sibling),
            device_id_type=MESH,
        ).wait_send()


def gather_weights(shards):
    rows = shards[0].shape[0]
    padded = [jnp.pad(shard, ((0, 0), (0, 2 * HALF - shard.shape[1]))) for shard in shards]
    any_spec = pl.BlockSpec(memory_space=pl.ANY)
    full = jax.ShapeDtypeStruct((BLOCKS * 2 * rows, HALF), jnp.bfloat16)
    return pl.pallas_call(
        functools.partial(gather_kernel, rows),
        out_shape=[full] * 3,
        in_specs=[any_spec] * 3,
        out_specs=[any_spec] * 3,
        scratch_shapes=[
            pltpu.SemaphoreType.DMA((3,)),
            pltpu.SemaphoreType.DMA((3,)),
            pltpu.SemaphoreType.DMA((3,)),
            pltpu.SemaphoreType.DMA((3,)),
            pltpu.SemaphoreType.DMA((3, BLOCKS)),
        ],
        compiler_params=pltpu.CompilerParams(collective_id=0, has_side_effects=True),
        name="gather_weights",
    )(*padded)


def from_behind(value, axis, steps):
    count = lax.axis_size(axis)
    return lax.ppermute(value, axis, [(source, source + steps) for source in range(count - steps)])


def rms_scale(values, gain):
    mean_square = jnp.mean(values * values, axis=-1, keepdims=True)
    return values * lax.rsqrt(mean_square + EPSILON) * gain


def segment_ids(positions, bounds):
    return jnp.sum((positions[:, None] >= bounds[None, :]).astype(jnp.int32), axis=1)


def short_conv(extended, segment_ext, conv_weight, count):
    taps = conv_weight.shape[0]
    own_segment = segment_ext[taps - 1 :]
    total = jnp.zeros((count, extended.shape[1]), jnp.float32)
    for tap_index in range(taps):
        first = taps - 1 - tap_index
        shifted = extended[first : first + count].astype(jnp.float32)
        same = (segment_ext[first : first + count] == own_segment).astype(jnp.float32)
        total = total + conv_weight[tap_index].astype(jnp.float32) * shifted * same[:, None]
    return total


def shards(
    tokens,
    lengths,
    attn_gain,
    w_query,
    w_key,
    w_value,
    w_outgate,
    gate_down,
    gate_up,
    gate_bias,
    conv_weight,
    head_gain,
    w_out,
    forward_norm_scale,
    w_gate,
    w_up,
    down_weight,
):
    gate_all, up_all, down_all = gather_weights((w_gate, w_up, down_weight))
    devices = lax.axis_size("seq")
    group_index = lax.axis_index("req")
    slice_index = lax.axis_index("seq")
    inputs = tokens[0]
    block_rows = inputs.shape[0]
    request_slots = lengths.shape[1]
    bounds_all = jnp.cumsum(lengths, axis=1)
    group_row = jnp.arange(lengths.shape[0], dtype=jnp.int32) == group_index
    bounds = jnp.sum(jnp.where(group_row[:, None], bounds_all, 0), axis=0)
    start_pos = slice_index * block_rows
    taps = conv_weight.shape[0]
    segment_ext = segment_ids(
        start_pos - (taps - 1) + jnp.arange(block_rows + taps - 1, dtype=jnp.int32), bounds
    )
    segment = segment_ext[taps - 1 :]
    segment_before = segment_ext[taps - 2]
    valid = segment < request_slots
    normed = rms_scale(inputs.astype(jnp.float32), attn_gain.astype(jnp.float32)).astype(
        jnp.bfloat16
    )
    projected = jnp.concatenate(
        [
            jnp.dot(normed, w_query, preferred_element_type=jnp.float32),
            jnp.dot(normed, w_key, preferred_element_type=jnp.float32),
            jnp.dot(normed, w_value, preferred_element_type=jnp.float32),
        ],
        axis=1,
    ).astype(jnp.bfloat16)
    outgate = jnp.dot(normed, w_outgate, preferred_element_type=jnp.float32)
    latent = jnp.dot(normed, gate_down, preferred_element_type=jnp.float32)
    logits = jnp.dot(latent, gate_up.astype(jnp.float32), precision=HIGHEST) + gate_bias
    log_decay = jax.nn.log_sigmoid(logits) / NORMALIZER
    previous = from_behind(projected[block_rows - (taps - 1) :], "seq", 1)
    extended = jnp.concatenate([previous, projected], axis=0)
    convolved = jax.nn.silu(short_conv(extended, segment_ext, conv_weight, block_rows)).astype(
        jnp.bfloat16
    )
    key_total = w_query.shape[1]
    value_total = w_value.shape[1]
    key_width = key_total // HEADS
    value_width = value_total // HEADS
    query = convolved[:, :key_total].astype(jnp.float32)
    keys = convolved[:, key_total : 2 * key_total].astype(jnp.float32)
    values = convolved[:, 2 * key_total :].reshape(block_rows, HEADS, value_width)

    order = jnp.arange(block_rows)
    lower = (order[:, None] >= order[None, :]).astype(jnp.float32)
    cumulative = jnp.dot(lower, log_decay, precision=HIGHEST)
    tail = cumulative[-1]
    keep = (segment == segment[-1]).astype(jnp.float32)
    keys_left = (keys * jnp.exp(tail[None] - cumulative) * keep[:, None]).reshape(
        block_rows, HEADS, key_width
    )
    state = jnp.einsum(
        "uhk,uhv->hkv", keys_left, values.astype(jnp.float32), precision=HIGHEST
    )
    decay = jnp.exp(tail) * (segment[-1] == segment_before).astype(jnp.float32)
    piece = key_total // devices
    pieces = state.astype(jnp.bfloat16).reshape(devices, piece, value_width)
    arrived = lax.all_to_all(pieces, "seq", split_axis=0, concat_axis=0, tiled=True)
    decays = lax.all_gather(decay, "seq").reshape(devices, devices, piece)
    mine = jnp.sum(
        jnp.where((jnp.arange(devices) == slice_index)[None, :, None], decays, 0.0), axis=1
    )
    before = [jnp.zeros((piece, value_width), jnp.float32)]
    for source in range(devices - 1):
        before.append(before[-1] * mine[source][:, None] + arrived[source].astype(jnp.float32))
    returned = lax.all_to_all(
        jnp.stack(before).astype(jnp.bfloat16), "seq", split_axis=0, concat_axis=0, tiled=True
    )
    incoming = returned.reshape(HEADS, key_width, value_width)

    allowed = (segment[:, None] == segment[None, :]) & (order[:, None] >= order[None, :])
    gap = jnp.where(allowed[:, :, None], cumulative[:, None] - cumulative[None, :], 0.0)
    products = query[:, None] * keys[None, :] * jnp.exp(gap)
    scores = jnp.sum(products.reshape(block_rows, block_rows, HEADS, key_width), axis=-1)
    scores = (scores * allowed[:, :, None].astype(jnp.float32)).astype(jnp.bfloat16)
    inner = jnp.einsum("tsh,shv->thv", scores, values, preferred_element_type=jnp.float32)
    clean = (segment == segment_before).astype(jnp.float32)
    query_decayed = (query * jnp.exp(cumulative) * clean[:, None]).reshape(
        block_rows, HEADS, key_width
    )
    carried = jnp.einsum(
        "thk,hkv->thv", query_decayed, incoming.astype(jnp.float32), precision=HIGHEST
    )
    attended = inner + carried
    gated = rms_scale(attended, head_gain.astype(jnp.float32)).reshape(
        block_rows, value_total
    ) * jax.nn.silu(outgate)
    resident = (
        jnp.dot(gated.astype(jnp.bfloat16), w_out, preferred_element_type=jnp.float32)
        + inputs.astype(jnp.float32)
    ).astype(jnp.bfloat16)

    mlp_normed = rms_scale(
        resident.astype(jnp.float32), forward_norm_scale.astype(jnp.float32)
    ).astype(jnp.bfloat16)
    swap = [(device, device ^ 1) for device in range(devices)]
    both_rows = jnp.concatenate([mlp_normed, lax.ppermute(mlp_normed, "seq", swap)], axis=0)
    width = inputs.shape[1]
    total = jnp.zeros((2 * block_rows, width), jnp.float32)
    gate_all, up_all, down_all = [
        full.reshape(SIDE, width, HALF) for full in (gate_all, up_all, down_all)
    ]
    for quarter in range(SIDE):
        gate = jnp.dot(both_rows, gate_all[quarter], preferred_element_type=jnp.float32)
        upward = jnp.dot(both_rows, up_all[quarter], preferred_element_type=jnp.float32)
        hidden = (jax.nn.silu(gate) * upward).astype(jnp.bfloat16)
        total = total + lax.dot_general(
            hidden, down_all[quarter], (((1,), (1,)), ((), ())), preferred_element_type=jnp.float32
        )
    other = lax.ppermute(total[block_rows:].astype(jnp.bfloat16), "seq", swap)
    mlp_own = (total[:block_rows] + other.astype(jnp.float32)).astype(jnp.bfloat16)
    output = jnp.where(
        valid[:, None], resident.astype(jnp.float32) + mlp_own.astype(jnp.float32), 0.0
    ).astype(jnp.bfloat16)
    return output[None]


def solution(mesh):
    return jax.shard_map(
        shards,
        mesh=mesh,
        in_specs=(P("req", "seq", None),) + (P(),) * 13 + (P("seq", "req"),) * 3,
        out_specs=P("req", "seq", None),
        check_vma=False,
    )
```

time: 451 us -> 257 us (0.57)
  waiting for transfers between devices: 261 us -> 7.35 us
  Pallas kernels: 0 us -> 79.4 us
  matrix products: 29.9 us -> 48.7 us
  between operations: 15.9 us -> 1.81 us
  local copies, waits for them, and re-layouts: 19.7 us -> 11.9 us
  other arithmetic: 71.9 us -> 65.2 us
  starting transfers between devices: 20.5 us -> 15.9 us
    all_gather x5 -> x0, waiting for transfers between devices: 195 us -> none  [the longest x1 84.9 us: prefix_2(): everything = jax.tree.map(lambda part: lax.all_gather(part, axis), shard)]
    pallas_call x0 -> x1, Pallas kernels: none -> 79.4 us  [gather_weights(): pl.pallas_call(functools.partial(gather_kernel, rows), out_shape=[full] *...]
    select_n x41 -> x0, other arithmetic: 50.1 us -> none  [the longest x32 47.7 us: lap(): return jax.tree.map(lambda a, b: jnp.where(reached, a, b), new, before)]
    unnamed x2 -> x30, other arithmetic: 0.01 us -> 39.6 us
    reduce_scatter x1 -> x0, waiting for transfers between devices: 37.1 us -> none  [swiglu_rows(): lax.psum_scatter(lax.dot_general(hidden, down_full, (((1,), (1,)), ((), (...]
    all_to_all x2, waiting for transfers between devices: 26.9 us -> 5.8 us  [the longest x1 5.8 us: shards(): lax.all_to_all(pieces, 'seq', split_axis=0, concat_axis=0, tiled=True)]
    dot_general x15 -> x13, matrix products: 20.4 us -> 38.2 us  [the longest x4 22.2 us: shards(): lax.dot_general(hidden, down_all[quarter], (((1,), (1,)), ((), ())), pref...]
    all_to_all x2, starting transfers between devices: 15.2 us -> 9.15 us  [the longest x1 5.29 us: shards(): lax.all_to_all(pieces, 'seq', split_axis=0, concat_axis=0, tiled=True)]
  transfers between devices with their start and end apart: 9 -> 5, of which waited for: 7 -> 2; matrix products, arithmetic and copies ran while one was open for 20% -> 11% of each run, Pallas kernels for 0% -> 31%
where the time goes in v1:
time: 257 us; the launch traced here: 254 us
  Pallas kernels  79.4 us (31%)
  other arithmetic  65.2 us (25%)
  matrix products  48.7 us (19%)
  blocking collectives  23.9 us (9%)
  starting transfers between devices  15.9 us (6%)
  local copies, waits for them, and re-layouts  11.9 us (5%)
  waiting for transfers between devices  7.35 us (3%)
    pallas_call x1, Pallas kernels, gather_weights(): pl.pallas_call(functools.partial(gather_kernel, rows), out_shape=[full] *...  79.4 us
    unnamed x30, other arithmetic  39.6 us
    all_gather x1, blocking collectives, shards(): decays = lax.all_gather(decay, 'seq').reshape(devices, devices, piece)  23.9 us
    dot_general x4, matrix products, shards(): lax.dot_general(hidden, down_all[quarter], (((1,), (1,)), ((), ())), pref...  22.2 us
    reduce_sum x1, other arithmetic, shards(): jnp.sum(products.reshape(block_rows, block_rows, HEADS, key_width), axis=-1)  12.3 us
    dot_general x4, matrix products, shards(): jnp.dot(both_rows, up_all[quarter], preferred_element_type=jnp.float32)  11.1 us
    all_to_all x1, waiting for transfers between devices, shards(): lax.all_to_all(pieces, 'seq', split_axis=0, concat_axis=0, tiled=True)  5.8 us
    dot_general x1, matrix products, shards(): jnp.dot(gated.astype(jnp.bfloat16), w_out, preferred_element_type=jnp.flo...  5.57 us
  transfers between devices with their start and end apart: 5, of which 2 were waited for; matrix products, arithmetic and copies ran while one was open for 11% of the time, Pallas kernels for 31%

profile of v1, /device:TPU:1, one launch (start us, length us, event | category | flops | bytes accessed | tf_op | source)
XLA Modules:
  0.0 254.1 jit_solution(7127067403263818362)
XLA Ops:
  0.0 1.4 fusion.25
  2.1 1.7 convolution_convert_fusion.2
  3.8 2.1 convolution_convert_fusion.3
  6.8 4.9 %collective-permute-start = (bf16[3,2048]{1,0:T(4,128)(2,1)S(1)}, bf16[3,2048]{1,0:T(4,128)(2,1)S(1)}, u32[]{:S(2)}, u32[]{:S(2)}) collective-permute-start(bf16[3,2048]{1,0:T(4,128)(2,1)S(1)} %slice.483), channel_id=1, source_target_pairs={{0,1},{1,2},{2,3},{3,4},{4,5},{5,6},{6,7},{7,8},{8,9},{9,10},{10,1... | collective-permute-start | bytes 36872 | tf_op jit(solution)/shard_map/ppermute | solution.py:197
  14.0 1.9 broadcast_compare_fusion
  17.7 23.9 %all-gather = f32[32,1,512]{2,1,0:T(1,128)S(1)} all-gather(f32[1,1,512]{2,1,0:T(1,128)S(1)} %get-tuple-element.73), channel_id=1, replica_groups=mesh['req'=4,'seq'=32] {'seq'}, dimensions={0}, use_global_device_ids=true | all-gather | bytes 67584 | tf_op jit(solution)/shard_map/all_gather | solution.py:301
  46.5 2.3 convolution_convert_fusion
  48.8 5.3 %all-to-all-start = ((bf16[32,16,512]{2,1,0:T(8,128)(2,1)}), bf16[32,16,512]{2,1,0:T(8,128)(2,1)S(1)}, u32[]{:S(2)}, u32[]{:S(2)}) async-start(bf16[32,16,512]{2,1,0:T(8,128)(2,1)} %bitcast.68), calls=%async_computation | async-start | bytes 1048576 | tf_op jit(solution)/shard_map/all_to_all | solution.py:300
  57.4 1.8 mul.977
  59.9 5.8 %all-to-all-done = bf16[32,16,512]{2,1,0:T(8,128)(2,1)S(1)} async-done(((bf16[32,16,512]{2,1,0:T(8,128)(2,1)}), bf16[32,16,512]{2,1,0:T(8,128)(2,1)S(1)}, u32[]{:S(2)}, u32[]{:S(2)}) %all-to-all-start) | async-done | bytes 524320 | tf_op jit(solution)/shard_map/all_to_all | solution.py:300
  71.8 1.4 constant_dynamic-update-slice_fusion.24
  75.9 1.3 constant_dynamic-update-slice_fusion.21
  77.2 1.4 constant_dynamic-update-slice_fusion.20
  78.6 1.4 constant_dynamic-update-slice_fusion.19
  80.0 1.4 constant_dynamic-update-slice_fusion.18
  81.4 1.4 constant_dynamic-update-slice_fusion.17
  82.8 1.4 constant_dynamic-update-slice_fusion.16
  84.2 1.4 constant_dynamic-update-slice_fusion.15
  85.6 1.4 constant_dynamic-update-slice_fusion.14
  87.0 1.4 constant_dynamic-update-slice_fusion.13
  88.4 1.4 constant_dynamic-update-slice_fusion.12
  89.8 1.4 constant_dynamic-update-slice_fusion.11
  91.2 1.4 constant_dynamic-update-slice_fusion.10
  92.7 1.4 constant_dynamic-update-slice_fusion.9
  94.1 1.4 constant_dynamic-update-slice_fusion.8
  95.5 1.4 constant_dynamic-update-slice_fusion.7
  96.9 1.4 constant_dynamic-update-slice_fusion.6
  98.3 1.4 constant_dynamic-update-slice_fusion.5
  99.7 1.4 constant_dynamic-update-slice_fusion.4
  101.1 1.4 constant_dynamic-update-slice_fusion.3
  102.5 1.4 constant_dynamic-update-slice_fusion.2
  103.9 1.4 constant_dynamic-update-slice_fusion.1
  105.3 1.4 constant_dynamic-update-slice_fusion
  106.7 3.9 %all-to-all-start.1 = ((bf16[32,16,512]{2,1,0:T(8,128)(2,1)}), bf16[32,16,512]{2,1,0:T(8,128)(2,1)S(1)}, u32[]{:S(2)}, u32[]{:S(2)}) async-start(bf16[32,16,512]{2,1,0:T(8,128)(2,1)} %constant_dynamic-update-slice_fusion), calls=%async_computation.1 | async-start | bytes 1048576 | tf_op jit(solution)/shard_map/all_to_all | solution.py:308
  110.6 12.3 %multiply_reduce_fusion = f32[128,128,2]{1,2,0:T(2,128)} fusion(f32[128,2,256]{2,0,1:T(8,128)} %bitcast.74, f32[128,2,256]{2,1,0:T(2,128)S(1)} %copy-done.7, f32[128,2,256]{2,0,1:T(8,128)} %bitcast.75, f32[128,2,256]{2,1,0:T(2,128)} %mul.977, pred[128,128]{1,0:T(8,128)(4,1)S(1)} %get-tuple-element.87), kind=kLoop, calls=%fused_computation | loop fusion | flops 41910272 | bytes 1196032 | tf_op jit(solution)/shard_map/reduce_sum | solution.py:316
  126.0 5.6 %multiply_reduce_fusion.1 = (f32[128]{0:T(128)S(1)}, f32[128,2048]{1,0:T(8,128)S(1)}) fusion(bf16[1,128,2048]{2,1,0:T(8,128)(2,1)} %param.17, bf16[1024,2048]{1,0:T(8,128)(2,1)} %param.29, f32[128,1024]{1,0:T(8,128)} %copy.69, bf16[2048,1024]{1,0:T(8,128)(2,1)} %param.23, f32[2048]{0:T(1024)S(1)} %convert_element_type.726, f32[128]{0:T(128)S(1)} %copy-done.39), kind=kOutput, calls=%fused_computation.47 | convolution fusion | flops 1077149568 | bytes 10494976 | tf_op jit(solution)/shard_map/dot_general | solution.py:331
  134.7 79.4 %gather_weights.1 = (bf16[8192,384]{1,0:T(8,128)(2,1)}, bf16[8192,384]{1,0:T(8,128)(2,1)}, bf16[8192,384]{1,0:T(8,128)(2,1)}) custom-call(bf16[64,768]{1,0:T(8,128)(2,1)} %pad.10.refs_0_, bf16[64,768]{1,0:T(8,128)(2,1)} %pad.11.refs_1_, bf16[64,768]{1,0:T(8,128)(2,1)} %pad.12.refs_2_), custom_call_target="tpu_custom_call" | custom-call | tf_op jit(solution)/shard_map/gather_weights/pallas_call | solution.py:178
  214.1 2.6 %fusion.3 = f32[256,384]{1,0:T(8,128)S(1)} fusion(bf16[8192,384]{1,0:T(8,128)(2,1)} %get-tuple-element.9, bf16[128,2048]{1,0:T(8,128)(2,1)} %collective-permute-done.1, bf16[128,2048]{1,0:T(8,128)(2,1)} %multiply_convert_fusion), kind=kOutput, calls=%fused_computation.10 | convolution fusion | flops 404750336 | bytes 3014656 | tf_op jit(solution)/shard_map/dot_general | solution.py:347
  216.7 3.2 %fusion.8 = f32[256,384]{1,0:T(8,128)} fusion(bf16[8192,384]{1,0:T(8,128)(2,1)} %get-tuple-element.9, bf16[128,2048]{1,0:T(8,128)(2,1)} %collective-permute-done.1, bf16[128,2048]{1,0:T(8,128)(2,1)} %multiply_convert_fusion), kind=kOutput, calls=%fused_computation.15 | convolution fusion | flops 404750336 | bytes 3014656 | tf_op jit(solution)/shard_map/dot_general | solution.py:347
  219.9 2.7 %fusion.13 = f32[256,384]{1,0:T(8,128)} fusion(bf16[8192,384]{1,0:T(8,128)(2,1)S(1)} %copy-done.40, bf16[128,2048]{1,0:T(8,128)(2,1)} %collective-permute-done.1, bf16[128,2048]{1,0:T(8,128)(2,1)} %multiply_convert_fusion), kind=kOutput, calls=%fused_computation.20 | convolution fusion | flops 404750336 | bytes 3014656 | tf_op jit(solution)/shard_map/dot_general | solution.py:347
  222.6 2.7 %fusion.19 = f32[256,384]{1,0:T(8,128)} fusion(bf16[8192,384]{1,0:T(8,128)(2,1)S(1)} %copy-done.40, bf16[128,2048]{1,0:T(8,128)(2,1)} %collective-permute-done.1, bf16[128,2048]{1,0:T(8,128)(2,1)} %multiply_convert_fusion), kind=kOutput, calls=%fused_computation.26 | convolution fusion | flops 404750336 | bytes 3014656 | tf_op jit(solution)/shard_map/dot_general | solution.py:347
  225.3 5.1 %fusion.17 = f32[256,2048]{1,0:T(8,128)} fusion(bf16[8192,384]{1,0:T(8,128)(2,1)} %get-tuple-element.10, f32[256,384]{1,0:T(8,128)} %fusion.19, bf16[8192,384]{1,0:T(8,128)(2,1)} %get-tuple-element.8, bf16[128,2048]{1,0:T(8,128)(2,1)} %collective-permute-done.1, bf16[128,2048]{1,0:T(8,128)(2,1)} %multiply_convert_fusion), kind=kOutput, calls=%fused_computation.24 | convolution fusion | flops 807993344 | bytes 6684672 | tf_op jit(solution)/shard_map/dot_general | solution.py:349
  230.3 5.7 %convolution_add_fusion.2 = f32[256,2048]{1,0:T(8,128)} fusion(f32[256,2048]{1,0:T(8,128)} %fusion.17, bf16[8192,384]{1,0:T(8,128)(2,1)} %get-tuple-element.10, f32[256,384]{1,0:T(8,128)} %fusion.13, bf16[8192,384]{1,0:T(8,128)(2,1)} %get-tuple-element.8, bf16[128,2048]{1,0:T(8,128)(2,1)} %collective-permute-done.1, bf16[128,2048]{1,0:T(8,128)(2,1)} %multiply_convert_fusion), kind=kOutput, calls=%fused_computation.3 | convolution fusion | flops 808517632 | bytes 8781824 | tf_op jit(solution)/shard_map/dot_general | solution.py:349
  236.1 5.7 %convolution_add_fusion.1 = f32[256,2048]{1,0:T(8,128)} fusion(f32[256,2048]{1,0:T(8,128)} %convolution_add_fusion.2, bf16[8192,384]{1,0:T(8,128)(2,1)} %get-tuple-element.10, f32[256,384]{1,0:T(8,128)} %fusion.8, bf16[8192,384]{1,0:T(8,128)(2,1)} %get-tuple-element.8, bf16[128,2048]{1,0:T(8,128)(2,1)} %collective-permute-done.1, ...), kind=kOutput, calls=%fused_computation.2 | convolution fusion | flops 808517632 | bytes 8781824 | tf_op jit(solution)/shard_map/dot_general | solution.py:349
  241.8 5.6 %convolution_add_fusion = f32[256,2048]{1,0:T(8,128)} fusion(f32[256,2048]{1,0:T(8,128)} %convolution_add_fusion.1, bf16[8192,384]{1,0:T(8,128)(2,1)} %get-tuple-element.10, f32[256,384]{1,0:T(8,128)S(1)} %fusion.3, bf16[8192,384]{1,0:T(8,128)(2,1)} %get-tuple-element.8, bf16[128,2048]{1,0:T(8,128)(2,1)} %collective-permute-done.1, ...), kind=kOutput, calls=%fused_computation.1 | convolution fusion | flops 808517632 | bytes 8781824 | tf_op jit(solution)/shard_map/dot_general | solution.py:349
  248.7 1.6 collective-permute-start.2
  250.4 1.5 collective-permute-done.2
  251.9 2.2 fusion.29
  (142 shorter events, 29.2 us)
Async XLA Ops:
  0.0 2.1 copy-start
  0.0 3.8 %copy-start.5 = (bf16[1,128,2048]{2,1,0:T(8,128)(2,1)S(1)}, bf16[1,128,2048]{2,1,0:T(8,128)(2,1)}, u32[]{:S(2)}) copy-start(bf16[1,128,2048]{2,1,0:T(8,128)(2,1)} %param.17) | copy-start | bytes 1572868
  1.4 14.6 %copy-start.38 = (f32[128]{0:T(128)}, f32[128]{0:T(128)S(1)}, u32[]{:S(2)}) copy-start(f32[128]{0:T(128)S(1)} %add_rsqrt_fusion.2) | copy-start | bytes 1540
  2.1 3.8 %copy-start.1 = (bf16[2048,1024]{1,0:T(8,128)(2,1)S(1)}, bf16[2048,1024]{1,0:T(8,128)(2,1)}, u32[]{:S(2)}) copy-start(bf16[2048,1024]{1,0:T(8,128)(2,1)} %param.22) | copy-start | bytes 12582916
  5.9 5.9 %copy-start.31 = (s32[4,4]{1,0:T(4,128)S(1)}, s32[4,4]{1,0:T(4,128)}, u32[]{:S(2)}) copy-start(s32[4,4]{1,0:T(4,128)} %param.18) | copy-start | bytes 196
  5.9 10.1 %copy-start.41 = (bf16[2048,16]{0,1:T(8,128)(2,1)S(1)}, bf16[2048,16]{0,1:T(8,128)(2,1)}, u32[]{:S(2)}) copy-start(bf16[2048,16]{0,1:T(8,128)(2,1)} %param.24) | copy-start | bytes 196612
  6.7 9.6 %copy-start.11 = (bf16[4,2048]{1,0:T(4,128)(2,1)S(1)}, bf16[4,2048]{1,0:T(4,128)(2,1)}, u32[]{:S(2)}) copy-start(bf16[4,2048]{1,0:T(4,128)(2,1)} %param.27) | copy-start | bytes 49156
  6.7 9.6 %copy-start.12 = (bf16[16,512]{1,0:T(8,128)(2,1)S(1)}, bf16[16,512]{1,0:T(8,128)(2,1)}, u32[]{:S(2)}) copy-start(bf16[16,512]{1,0:T(8,128)(2,1)} %param.25) | copy-start | bytes 49156
  6.7 9.6 %copy-start.28 = (f32[512]{0:T(512)S(1)}, f32[512]{0:T(512)}, u32[]{:S(2)}) copy-start(f32[512]{0:T(512)} %param.26) | copy-start | bytes 6148
  6.8 37.0 %collective-permute-start = (bf16[3,2048]{1,0:T(4,128)(2,1)S(1)}, bf16[3,2048]{1,0:T(4,128)(2,1)S(1)}, u32[]{:S(2)}, u32[]{:S(2)}) collective-permute-start(bf16[3,2048]{1,0:T(4,128)(2,1)S(1)} %slice.483), channel_id=1, source_target_pairs={{0,1},{1,2},{2,3},{3,4},{4,5},{5,6},{6,7},{7,8},{8,9},{9,10},{10,1... | collective-permute-start | bytes 36872 | tf_op jit(solution)/shard_map/ppermute | solution.py:197
  16.3 27.7 %copy-start.34 = (f32[128]{0:T(128)S(1)}, f32[128]{0:T(128)}, u32[]{:S(2)}) copy-start(f32[128]{0:T(128)} %get-tuple-element.81) | copy-start | bytes 1540
  16.3 27.7 %copy-start.35 = (f32[128]{0:T(128)S(1)}, f32[128]{0:T(128)}, u32[]{:S(2)}) copy-start(f32[128]{0:T(128)} %get-tuple-element.82) | copy-start | bytes 1540
  16.3 27.7 %copy-start.36 = (f32[128]{0:T(128)S(1)}, f32[128]{0:T(128)}, u32[]{:S(2)}) copy-start(f32[128]{0:T(128)} %get-tuple-element.83) | copy-start | bytes 1540
  43.8 1.0 copy-start.15
  43.8 1.0 copy-start.26
  43.8 1.0 copy-start.27
  44.8 4.0 %copy-start.3 = (bf16[128,1024]{1,0:T(8,128)(2,1)}, bf16[128,1024]{1,0:T(8,128)(2,1)S(1)}, u32[]{:S(2)}) copy-start(bf16[128,1024]{1,0:T(8,128)(2,1)S(1)} %slice.487) | copy-start | bytes 786436
  44.9 10.8 %copy-start.37 = (bf16[512]{0:T(512)(128)(2,1)S(1)}, bf16[512]{0:T(512)(128)(2,1)}, u32[]{:S(2)}) copy-start(bf16[512]{0:T(512)(128)(2,1)} %param.28) | copy-start | bytes 3076
  44.9 10.8 %copy-start.25 = (bf16[2048]{0:T(1024)(128)(2,1)S(1)}, bf16[2048]{0:T(1024)(128)(2,1)}, u32[]{:S(2)}) copy-start(bf16[2048]{0:T(1024)(128)(2,1)} %param.30) | copy-start | bytes 12292
  48.8 17.7 %copy-start.13 = (f32[16]{0:T(128)S(1)}, f32[16]{0:T(128)}, u32[]{:S(2)}) copy-start(f32[16]{0:T(128)} %get-tuple-element.40) | copy-start | bytes 196
  48.8 18.4 %copy-start.14 = (f32[16]{0:T(128)S(1)}, f32[16]{0:T(128)}, u32[]{:S(2)}) copy-start(f32[16]{0:T(128)} %get-tuple-element.39) | copy-start | bytes 196
  48.8 16.9 %all-to-all-start = ((bf16[32,16,512]{2,1,0:T(8,128)(2,1)}), bf16[32,16,512]{2,1,0:T(8,128)(2,1)S(1)}, u32[]{:S(2)}, u32[]{:S(2)}) async-start(bf16[32,16,512]{2,1,0:T(8,128)(2,1)} %bitcast.68), calls=%async_computation | async-start | bytes 1048576 | tf_op jit(solution)/shard_map/all_to_all | solution.py:300
  54.8 28.0 %copy-start.23 = (f32[16]{0:T(128)S(1)}, f32[16]{0:T(128)}, u32[]{:S(2)}) copy-start(f32[16]{0:T(128)} %get-tuple-element.28) | copy-start | bytes 196
  54.8 29.4 %copy-start.22 = (f32[16]{0:T(128)S(1)}, f32[16]{0:T(128)}, u32[]{:S(2)}) copy-start(f32[16]{0:T(128)} %get-tuple-element.26) | copy-start | bytes 196
  55.7 31.3 %copy-start.21 = (f32[16]{0:T(128)S(1)}, f32[16]{0:T(128)}, u32[]{:S(2)}) copy-start(f32[16]{0:T(128)} %get-tuple-element.24) | copy-start | bytes 196
  55.7 34.1 %copy-start.20 = (f32[16]{0:T(128)S(1)}, f32[16]{0:T(128)}, u32[]{:S(2)}) copy-start(f32[16]{0:T(128)} %get-tuple-element.22) | copy-start | bytes 196
  55.7 36.9 %copy-start.19 = (f32[16]{0:T(128)S(1)}, f32[16]{0:T(128)}, u32[]{:S(2)}) copy-start(f32[16]{0:T(128)} %get-tuple-element.20) | copy-start | bytes 196
  56.5 39.0 %copy-start.18 = (f32[16]{0:T(128)S(1)}, f32[16]{0:T(128)}, u32[]{:S(2)}) copy-start(f32[16]{0:T(128)} %get-tuple-element.18) | copy-start | bytes 196
  56.5 41.8 %copy-start.17 = (f32[16]{0:T(128)S(1)}, f32[16]{0:T(128)}, u32[]{:S(2)}) copy-start(f32[16]{0:T(128)} %get-tuple-element.16) | copy-start | bytes 196
  56.6 44.5 %copy-start.16 = (f32[16]{0:T(128)S(1)}, f32[16]{0:T(128)}, u32[]{:S(2)}) copy-start(f32[16]{0:T(128)} %get-tuple-element.14) | copy-start | bytes 196
  57.3 42.3 %copy-start.30 = (f32[16]{0:T(128)S(1)}, f32[16]{0:T(128)}, u32[]{:S(2)}) copy-start(f32[16]{0:T(128)} %get-tuple-element.15) | copy-start | bytes 196
  57.4 45.2 %copy-start.29 = (f32[16]{0:T(128)S(1)}, f32[16]{0:T(128)}, u32[]{:S(2)}) copy-start(f32[16]{0:T(128)} %get-tuple-element.13) | copy-start | bytes 196
  57.4 46.6 %copy-start.24 = (f32[16]{0:T(128)S(1)}, f32[16]{0:T(128)}, u32[]{:S(2)}) copy-start(f32[16]{0:T(128)} %get-tuple-element.12) | copy-start | bytes 196
  57.4 48.0 %copy-start.32 = (f32[16]{0:T(128)S(1)}, f32[16]{0:T(128)}, u32[]{:S(2)}) copy-start(f32[16]{0:T(128)} %get-tuple-element.11) | copy-start | bytes 196
  59.2 51.4 %copy-start.7 = (f32[128,2,256]{2,1,0:T(2,128)S(1)}, f32[128,2,256]{2,1,0:T(2,128)}, u32[]{:S(2)}) copy-start(f32[128,2,256]{2,1,0:T(2,128)} %sub.30) | copy-start | bytes 786436
  65.7 12.8 %copy-start.2 = (bf16[32,16,512]{2,1,0:T(8,128)(2,1)}, bf16[32,16,512]{2,1,0:T(8,128)(2,1)S(1)}, u32[]{:S(2)}) copy-start(bf16[32,16,512]{2,1,0:T(8,128)(2,1)S(1)} %all-to-all-done) | copy-start | bytes 1572868
  106.7 16.2 %all-to-all-start.1 = ((bf16[32,16,512]{2,1,0:T(8,128)(2,1)}), bf16[32,16,512]{2,1,0:T(8,128)(2,1)S(1)}, u32[]{:S(2)}, u32[]{:S(2)}) async-start(bf16[32,16,512]{2,1,0:T(8,128)(2,1)} %constant_dynamic-update-slice_fusion), calls=%async_computation.1 | async-start | bytes 1048576 | tf_op jit(solution)/shard_map/all_to_all | solution.py:308
  110.6 12.3 %copy-start.6 = (f32[128,512]{1,0:T(8,128)S(1)}, f32[128,512]{1,0:T(8,128)}, u32[]{:S(2)}) copy-start(f32[128,512]{1,0:T(8,128)} %get-tuple-element.68) | copy-start | bytes 786436
  110.6 13.0 %copy-start.4 = (bf16[128,1024]{1,0:T(8,128)(2,1)S(1)}, bf16[128,1024]{1,0:T(8,128)(2,1)}, u32[]{:S(2)}) copy-start(bf16[128,1024]{1,0:T(8,128)(2,1)} %copy-done.3) | copy-start | bytes 786436
  123.6 2.4 copy-start.39
  126.0 6.7 %copy-start.8 = (bf16[64,704]{1,0:T(8,128)(2,1)S(1)}, bf16[64,704]{1,0:T(8,128)(2,1)}, u32[]{:S(2)}) copy-start(bf16[64,704]{1,0:T(8,128)(2,1)} %param.31) | copy-start | bytes 270340
  126.0 7.4 %copy-start.9 = (bf16[64,704]{1,0:T(8,128)(2,1)S(1)}, bf16[64,704]{1,0:T(8,128)(2,1)}, u32[]{:S(2)}) copy-start(bf16[64,704]{1,0:T(8,128)(2,1)} %param.32) | copy-start | bytes 270340
  126.0 8.0 %copy-start.10 = (bf16[64,704]{1,0:T(8,128)(2,1)S(1)}, bf16[64,704]{1,0:T(8,128)(2,1)}, u32[]{:S(2)}) copy-start(bf16[64,704]{1,0:T(8,128)(2,1)} %param.33) | copy-start | bytes 270340
  132.5 81.6 %collective-permute-start.1 = (bf16[128,2048]{1,0:T(8,128)(2,1)}, bf16[128,2048]{1,0:T(8,128)(2,1)}, u32[]{:S(2)}, u32[]{:S(2)}) collective-permute-start(bf16[128,2048]{1,0:T(8,128)(2,1)} %multiply_convert_fusion), channel_id=1, source_target_pairs={{0,1},{1,0},{2,3},{3,2},{4,5},{5,4},{6,7},{7,6},{8,9},{9,8},{10,11... | collective-permute-start | bytes 1572872 | tf_op jit(solution)/shard_map/ppermute | solution.py:339
  214.1 5.8 %copy-start.40 = (bf16[8192,384]{1,0:T(8,128)(2,1)S(1)}, bf16[8192,384]{1,0:T(8,128)(2,1)}, u32[]{:S(2)}) copy-start(bf16[8192,384]{1,0:T(8,128)(2,1)} %get-tuple-element.9) | copy-start | bytes 18874372
  241.8 10.1 %copy-start.33 = (pred[128]{0:T(512)(128)(4,1)S(1)}, pred[128]{0:T(512)(128)(4,1)}, u32[]{:S(2)}) copy-start(pred[128]{0:T(512)(128)(4,1)} %get-tuple-element.78) | copy-start | bytes 388
  248.7 3.2 %collective-permute-start.2 = (bf16[128,2048]{1,0:T(8,128)(2,1)S(1)}, bf16[128,2048]{1,0:T(8,128)(2,1)S(1)}, u32[]{:S(2)}, u32[]{:S(2)}) collective-permute-start(bf16[128,2048]{1,0:T(8,128)(2,1)S(1)} %slice.723), channel_id=1, source_target_pairs={{0,1},{1,0},{2,3},{3,2},{4,5},{5,4},{6,7},{7,6},{8,9},{9,8},{10,11... | collective-permute-start | bytes 1572872 | tf_op jit(solution)/shard_map/ppermute | solution.py:352

commit v2 on v1

v2 whole, which is shorter than its diff:
```python
import jax
import jax.numpy as jnp
from jax import lax
from jax.experimental import pallas as pl
from jax.experimental.pallas import tpu as pltpu
from jax.sharding import PartitionSpec as P

HEADS = 2
EPSILON = 1e-05
NORMALIZER = 16.0
HIGHEST = lax.Precision.HIGHEST
MESH = pl.DeviceIdType.MESH
F32 = jnp.float32
BF16 = jnp.bfloat16

SIDE = 4
BLOCKS = SIDE**3
DEVICES = 2 * SIDE * SIDE
HALF = 384
ROWS = 128
SUB = 16
HALO = 16
WIDTH = 2048
KEYS = 512
VALUES = 1024
KW = KEYS // HEADS
VW = VALUES // HEADS
PIECE = KEYS // DEVICES
ORDERS = (("x", "y", "z"), ("z", "x", "y"), ("y", "z", "x"))
KEEP, CLEAN, VALID = 4, 5, 6


def place():
    seq = lax.axis_index("seq")
    return {
        "x": seq // (2 * SIDE),
        "z": (seq // 2) % SIDE,
        "y": lax.axis_index("req"),
        "c": seq % 2,
    }


def device_at(at):
    return (at["y"], (at["x"] * SIDE + at["z"]) * 2 + at["c"])


def moved(at, axis, by):
    new = dict(at)
    new[axis] = (at[axis] + by + SIDE) % SIDE
    return new


def dot(a, b):
    return jnp.dot(a, b, preferred_element_type=F32)


def dot_nt(a, b):
    return lax.dot_general(a, b, (((1,), (1,)), ((), ())), preferred_element_type=F32)


def split(a):
    high = a.astype(BF16)
    return high, (a - high.astype(F32)).astype(BF16)


def silu(a):
    return a * jax.nn.sigmoid(a)


def layer_kernel(
    tokens,
    attn_gain,
    gate_down,
    gate_up,
    gate_bias,
    conv_weight,
    head_gain,
    forward_scale,
    masks,
    allowed,
    w_query,
    w_key,
    w_value,
    w_outgate,
    w_out_hbm,
    gate_shard,
    up_shard,
    down_shard,
    out,
    wg,
    wu,
    wd,
    staged,
    w_attn,
    w_out,
    normed,
    proj,
    outgate,
    query,
    keys,
    values,
    total,
    state_out,
    decay_out,
    state_in,
    decay_in,
    before,
    incoming,
    scores,
    gated,
    resident,
    x_rows,
    hidden,
    acc,
    other_send,
    other_recv,
    load_sem,
    local_sem,
    pair_send,
    pair_recv,
    send_sem,
    recv_sem,
    halo_sem,
    state_sem,
    swap_sem,
):
    me = place()
    core = me["c"]
    seq = lax.axis_index("seq")
    req = lax.axis_index("req")
    sibling = dict(me, c=1 - core)
    onward = 1 - 2 * core

    loads = []
    for index, (source, first, count) in enumerate(
        (
            (w_query, 0, KEYS),
            (w_key, KEYS, KEYS),
            (w_value, 2 * KEYS, VALUES),
            (w_outgate, 2 * KEYS + VALUES, VALUES),
        )
    ):
        load = pltpu.make_async_copy(
            source, w_attn.at[:, pl.ds(first, count)], load_sem.at[index]
        )
        load.start()
        loads.append(load)
    load_out = pltpu.make_async_copy(w_out_hbm, w_out, load_sem.at[4])
    load_out.start()

    barrier = pltpu.get_barrier_semaphore()

    def greet(step, carry):
        pl.semaphore_signal(
            barrier, inc=1, device_id=(req, (seq + step) % DEVICES), device_id_type=MESH
        )
        return carry

    lax.fori_loop(1, DEVICES, greet, 0)
    for by in (1, -1):
        pl.semaphore_signal(
            barrier, inc=1, device_id=device_at(moved(me, "y", by)), device_id_type=MESH
        )
    pl.semaphore_wait(barrier, DEVICES + 1)

    def slot(part, at):
        column = at["x"] * SIDE + at["z"]
        if part == 2:
            return wd.at[
                pl.ds(pl.multiple_of(at["y"] * HALF, 128), HALF),
                pl.ds(pl.multiple_of(column * 128, 128), 128),
            ]
        block = at["y"] * (SIDE * SIDE) + column
        return (wg, wu)[part].at[pl.ds(pl.multiple_of(block * 128, 128), 128), :]

    def own_half(part, source_core):
        if part == 2:
            return staged.at[pl.ds(pl.multiple_of(source_core * 64, 64), 64), :]
        block = (me["y"] * SIDE + me["x"]) * SIDE + me["z"]
        first = pl.multiple_of(block * 128 + source_core * 64, 64)
        return (wg, wu)[part].at[pl.ds(first, 64), :]

    locals_, pairs = [], []
    for part, shard in enumerate((gate_shard, up_shard, down_shard)):
        pair = pltpu.make_async_remote_copy(
            src_ref=shard.at[:, pl.ds(pl.multiple_of((1 - core) * HALF, 128), HALF)],
            dst_ref=own_half(part, core),
            send_sem=pair_send.at[part],
            recv_sem=pair_recv.at[part],
            device_id=device_at(sibling),
            device_id_type=MESH,
        )
        pair.start()
        pairs.append(pair)
        own = pltpu.make_async_copy(
            shard.at[:, pl.ds(pl.multiple_of(core * HALF, 128), HALF)],
            own_half(part, core),
            local_sem.at[part],
        )
        own.start()
        locals_.append(own)

    def block_of(at):
        return (at["y"] * SIDE + at["x"]) * SIDE + at["z"]

    def copy_of(part, at, axis, by):
        return pltpu.make_async_remote_copy(
            src_ref=slot(part, at),
            dst_ref=slot(part, at),
            send_sem=send_sem.at[part],
            recv_sem=recv_sem.at[part, block_of(at)],
            device_id=device_at(moved(me, axis, by)),
            device_id_type=MESH,
        )

    def send(part, at, axis, by):
        copy_of(part, at, axis, by).start()

    def both(part, at, axis):
        send(part, at, axis, 1)
        send(part, at, axis, -1)

    def arrive(part, at):
        copy_of(part, at, "x", 1).wait_recv()

    kinds = (-onward, onward, 2)

    def at_of(part, *steps):
        at = dict(me)
        for axis, by in zip(ORDERS[part], steps):
            at[axis] = (me[axis] + by + SIDE) % SIDE
        return at

    def first_axis(kind):
        for part in range(3):
            at = at_of(part, kinds[kind])
            arrive(part, at)
            if kind == 0:
                send(part, at, ORDERS[part][0], onward)
            both(part, at, ORDERS[part][1])
            both(part, at, ORDERS[part][2])

    def second_axis(kind):
        def step_(step, carry):
            for part in range(3):
                at = at_of(part, step, kinds[kind])
                arrive(part, at)
                if kind == 0:
                    send(part, at, ORDERS[part][1], onward)
                both(part, at, ORDERS[part][2])
            return carry

        lax.fori_loop(0, SIDE, step_, 0)

    def third_axis(kind, second, parts=(0, 1, 2)):
        def step_(step, carry):
            for part in parts:
                at = at_of(part, step, second, kinds[kind])
                arrive(part, at)
                if kind == 0:
                    send(part, at, ORDERS[part][2], onward)
            return carry

        lax.fori_loop(0, SIDE, step_, 0)

    inputs = tokens[...].astype(F32)
    mean_square = jnp.mean(inputs * inputs, axis=-1, keepdims=True)
    normed[...] = (
        inputs * lax.rsqrt(mean_square + EPSILON) * attn_gain[...].astype(F32)
    ).astype(BF16)

    for part in range(3):
        locals_[part].wait()
        pairs[part].wait_recv()
        if part == 2:
            ref = slot(2, me)
            ref[...] = jnp.transpose(staged[...].astype(F32)).astype(BF16)
        both(part, me, ORDERS[part][0])
    for part in range(3):
        both(part, me, ORDERS[part][1])
    for part in range(3):
        both(part, me, ORDERS[part][2])

    def project(index, carry):
        columns = pl.ds(pl.multiple_of(index * 256, 256), 256)
        proj[pl.ds(HALO, ROWS), columns] = dot(normed[...], w_attn[:, columns]).astype(BF16)
        return carry

    loads[0].wait()
    loads[1].wait()
    lax.fori_loop(0, 4, project, 0)
    loads[2].wait()
    lax.fori_loop(4, 8, project, 0)
    halo = pltpu.make_async_remote_copy(
        src_ref=proj.at[pl.ds(ROWS, HALO), :],
        dst_ref=proj.at[pl.ds(0, HALO), :],
        send_sem=halo_sem.at[0],
        recv_sem=halo_sem.at[1],
        device_id=(req, (seq + 1) % DEVICES),
        device_id_type=MESH,
    )
    halo.start()

    for kind in range(3):
        first_axis(kind)

    def project_gate(index, carry):
        source = pl.ds(pl.multiple_of(index * 256 + 2 * KEYS + VALUES, 256), 256)
        target = pl.ds(pl.multiple_of(index * 256, 256), 256)
        outgate[:, target] = dot(normed[...], w_attn[:, source])
        return carry

    loads[3].wait()
    lax.fori_loop(0, 4, project_gate, 0)
    latent = dot(normed[...], gate_down[...])
    logits = (
        jnp.dot(latent, gate_up[...].astype(F32), precision=HIGHEST, preferred_element_type=F32)
        + gate_bias[...]
    )
    log_decay = (jnp.minimum(logits, 0.0) - jnp.log1p(jnp.exp(-jnp.abs(logits)))) / NORMALIZER
    row = lax.broadcasted_iota(jnp.int32, (ROWS, ROWS), 0)
    lane = lax.broadcasted_iota(jnp.int32, (ROWS, ROWS), 1)
    lower = (row >= lane).astype(F32)
    cumulative = jnp.dot(lower, log_decay, precision=HIGHEST, preferred_element_type=F32)
    total[...] = cumulative.reshape(ROWS // SUB, SUB, KEYS)
    table = masks[...]
    clean_block = table[ROWS - 1 : ROWS, CLEAN : CLEAN + 1]
    tail_rows = jnp.dot(
        jnp.transpose(log_decay), jnp.ones((ROWS, 128), F32), precision=HIGHEST,
        preferred_element_type=F32,
    )
    decay_out[...] = jnp.exp(tail_rows) * clean_block

    halo.wait()
    for chunk in range(4):
        columns = slice(chunk * 512, (chunk + 1) * 512)
        rows = proj[:, columns].astype(F32)
        taps = conv_weight[:, columns].astype(F32)
        mixed = rows[HALO:] * taps[0:1]
        for tap in range(1, 4):
            shifted = pltpu.roll(rows, tap, 0)[HALO:]
            same = table[:, tap : tap + 1]
            mixed = mixed + taps[tap : tap + 1] * jnp.where(same > 0.0, shifted, 0.0)
        mixed = silu(mixed).astype(BF16)
        if chunk == 0:
            query[...] = mixed.astype(F32).reshape(ROWS // SUB, SUB, KEYS)
        elif chunk == 1:
            keys[...] = mixed.astype(F32).reshape(ROWS // SUB, SUB, KEYS)
        else:
            values[:, (chunk - 2) * 512 : (chunk - 1) * 512] = mixed

    tail = cumulative[ROWS - 1 : ROWS]
    keys_left = (
        keys[...].reshape(ROWS, KEYS) * jnp.exp(tail - cumulative) * table[:, KEEP : KEEP + 1]
    )
    for head in range(HEADS):
        high, low = split(jnp.transpose(keys_left[:, head * KW : (head + 1) * KW]))
        head_values = values[:, head * VW : (head + 1) * VW]
        state_out[head * KW : (head + 1) * KW, :] = (
            dot(high, head_values) + dot(low, head_values)
        ).astype(BF16)

    def piece_of(ref, index):
        return ref.at[pl.ds(pl.multiple_of(index * PIECE, PIECE), PIECE), :]

    def exchange(source, target, which):
        def step_(step, carry):
            to = (seq + step) % DEVICES
            pltpu.make_async_remote_copy(
                src_ref=piece_of(source, to),
                dst_ref=piece_of(target, seq),
                send_sem=state_sem.at[2 * which],
                recv_sem=state_sem.at[2 * which + 1],
                device_id=(req, to),
                device_id_type=MESH,
            ).start()
            return carry

        lax.fori_loop(1, DEVICES, step_, 0)

    def exchanged(source, target, which):
        count = (DEVICES - 1) * PIECE
        return pltpu.make_async_remote_copy(
            src_ref=source.at[pl.ds(0, count), :],
            dst_ref=target.at[pl.ds(0, count), :],
            send_sem=state_sem.at[2 * which],
            recv_sem=state_sem.at[2 * which + 1],
            device_id=device_at(sibling),
            device_id_type=MESH,
        )

    exchange(decay_out, decay_in, 0)
    exchange(state_out, state_in, 1)
    mine = pl.ds(pl.multiple_of(seq * PIECE, PIECE), PIECE)
    decay_in[mine, :] = decay_out[mine, :]
    state_in[mine, :] = state_out[mine, :]

    second_axis(0)

    scores[...] = jnp.zeros_like(scores)
    sub_row = row // SUB

    def diagonal(step, carry):
        key_row = keys[:, pl.ds(step, 1), :]
        total_row = total[:, pl.ds(step, 1), :]
        product = query[...] * key_row * jnp.exp(jnp.minimum(total[...] - total_row, 0.0))
        here = lane == sub_row * SUB + step
        for head in range(HEADS):
            summed = jnp.sum(product[:, :, head * KW : (head + 1) * KW], axis=-1, keepdims=True)
            scores[head] += jnp.where(here, summed.reshape(ROWS, 1), 0.0)
        return carry

    lax.fori_loop(0, SUB, diagonal, 0)
    flat_keys = keys[...].reshape(ROWS, KEYS)
    for sub in range(1, ROWS // SUB):
        base = total[sub - 1, SUB - 1 : SUB, :]
        query_high, query_low = split(query[sub] * jnp.exp(total[sub] - base))
        key_high, key_low = split(flat_keys * jnp.exp(jnp.minimum(base - cumulative, 0.0)))
        for head in range(HEADS):
            part = slice(head * KW, (head + 1) * KW)
            block = (
                dot_nt(query_high[:, part], key_high[:, part])
                + dot_nt(query_high[:, part], key_low[:, part])
                + dot_nt(query_low[:, part], key_high[:, part])
            )
            rows = slice(sub * SUB, (sub + 1) * SUB)
            scores[head, rows, :] += jnp.where(lane[:SUB] < sub * SUB, block, 0.0)

    exchanged(decay_out, decay_in, 0).wait_recv()
    exchanged(state_out, state_in, 1).wait_recv()

    def prefix(step, running):
        rows = pl.ds(pl.multiple_of(step * PIECE, PIECE), PIECE)
        before[rows, :] = running.astype(BF16)
        decay = decay_in[rows, :]
        decay = jnp.concatenate([decay] * (VW // 128), axis=1)
        return running * decay + state_in[rows, :].astype(F32)

    lax.fori_loop(0, DEVICES, prefix, jnp.zeros((PIECE, VW), F32))
    exchange(before, incoming, 2)
    incoming[mine, :] = before[mine, :]

    second_axis(1)
    second_axis(2)
    third_axis(0, 0)

    exchanged(before, incoming, 2).wait_recv()
    query_decayed = (
        query[...].reshape(ROWS, KEYS) * jnp.exp(cumulative) * table[:, CLEAN : CLEAN + 1]
    )
    for head in range(HEADS):
        key_part = slice(head * KW, (head + 1) * KW)
        value_part = slice(head * VW, (head + 1) * VW)
        high, low = split(query_decayed[:, key_part])
        weights = (scores[head] * allowed[...]).astype(BF16)
        before_state = incoming[key_part, :]
        attended = (
            dot(weights, values[:, value_part]) + dot(high, before_state) + dot(low, before_state)
        )
        mean_square = jnp.mean(attended * attended, axis=-1, keepdims=True)
        scaled = attended * lax.rsqrt(mean_square + EPSILON) * head_gain[...].astype(F32)
        gated[:, value_part] = (scaled * silu(outgate[:, value_part])).astype(BF16)

    load_out.wait()

    def project_out(index, carry):
        columns = pl.ds(pl.multiple_of(index * 256, 256), 256)
        resident[:, columns] = (
            dot(gated[...], w_out[:, columns]) + tokens[:, columns].astype(F32)
        ).astype(BF16)
        return carry

    lax.fori_loop(0, WIDTH // 256, project_out, 0)
    wide = resident[...].astype(F32)
    mean_square = jnp.mean(wide * wide, axis=-1, keepdims=True)
    own_rows = pl.ds(pl.multiple_of(core * ROWS, ROWS), ROWS)
    other_rows = pl.ds(pl.multiple_of((1 - core) * ROWS, ROWS), ROWS)
    x_rows[own_rows, :] = (
        wide * lax.rsqrt(mean_square + EPSILON) * forward_scale[...].astype(F32)
    ).astype(BF16)
    swap_x = pltpu.make_async_remote_copy(
        src_ref=x_rows.at[own_rows, :],
        dst_ref=x_rows.at[own_rows, :],
        send_sem=swap_sem.at[0],
        recv_sem=swap_sem.at[1],
        device_id=device_at(sibling),
        device_id_type=MESH,
    )
    swap_x.start()

    for second in kinds:
        third_axis(0, second)
    for second in (0,) + kinds:
        third_axis(1, second)
        third_axis(2, second)
    swap_x.wait()

    for quarter in range(SIDE):
        columns = slice(quarter * HALF, (quarter + 1) * HALF)
        features = slice(quarter * WIDTH, (quarter + 1) * WIDTH)
        gate = dot(x_rows[...], wg[features, :])
        upward = dot(x_rows[...], wu[features, :])
        hidden[:, columns] = (silu(gate) * upward).astype(BF16)

    def project_down(index, carry):
        columns = pl.ds(pl.multiple_of(index * 256, 256), 256)
        acc[:, columns] = dot(hidden[...], wd[:, columns])
        return carry

    lax.fori_loop(0, WIDTH // 256, project_down, 0)
    other_send[...] = acc[other_rows, :].astype(BF16)
    swap_out = pltpu.make_async_remote_copy(
        src_ref=other_send,
        dst_ref=other_recv,
        send_sem=swap_sem.at[2],
        recv_sem=swap_sem.at[3],
        device_id=device_at(sibling),
        device_id_type=MESH,
    )
    swap_out.start()
    swap_out.wait()
    mlp = (acc[own_rows, :] + other_recv[...].astype(F32)).astype(BF16)
    result = resident[...].astype(F32) + mlp.astype(F32)
    out[...] = jnp.where(table[:, VALID : VALID + 1] > 0.0, result, 0.0).astype(BF16)

    exchanged(decay_out, decay_in, 0).wait_send()
    exchanged(state_out, state_in, 1).wait_send()
    exchanged(before, incoming, 2).wait_send()
    for part in range(3):
        pairs[part].wait_send()
        sent = wg.at[pl.ds(0, (BLOCKS - 1) * 128), :]
        pltpu.make_async_remote_copy(
            src_ref=sent,
            dst_ref=sent,
            send_sem=send_sem.at[part],
            recv_sem=recv_sem.at[part, 0],
            device_id=device_at(sibling),
            device_id_type=MESH,
        ).wait_send()


def layer(vmem_args, hbm_args):
    vmem = pl.BlockSpec(memory_space=pltpu.VMEM)
    hbm = pl.BlockSpec(memory_space=pl.ANY)
    dma = pltpu.SemaphoreType.DMA
    return pl.pallas_call(
        layer_kernel,
        out_shape=jax.ShapeDtypeStruct((ROWS, WIDTH), BF16),
        in_specs=[vmem] * len(vmem_args) + [hbm] * len(hbm_args),
        out_specs=vmem,
        scratch_shapes=[
            pltpu.VMEM((BLOCKS * 128, HALF), BF16),
            pltpu.VMEM((BLOCKS * 128, HALF), BF16),
            pltpu.VMEM((SIDE * HALF, WIDTH), BF16),
            pltpu.VMEM((128, HALF), BF16),
            pltpu.VMEM((WIDTH, 2 * KEYS + 2 * VALUES), BF16),
            pltpu.VMEM((VALUES, WIDTH), BF16),
            pltpu.VMEM((ROWS, WIDTH), BF16),
            pltpu.VMEM((HALO + ROWS, 2 * KEYS + VALUES), BF16),
            pltpu.VMEM((ROWS, VALUES), F32),
            pltpu.VMEM((ROWS // SUB, SUB, KEYS), F32),
            pltpu.VMEM((ROWS // SUB, SUB, KEYS), F32),
            pltpu.VMEM((ROWS, VALUES), BF16),
            pltpu.VMEM((ROWS // SUB, SUB, KEYS), F32),
            pltpu.VMEM((KEYS, VW), BF16),
            pltpu.VMEM((KEYS, 128), F32),
            pltpu.VMEM((KEYS, VW), BF16),
            pltpu.VMEM((KEYS, 128), F32),
            pltpu.VMEM((KEYS, VW), BF16),
            pltpu.VMEM((KEYS, VW), BF16),
            pltpu.VMEM((HEADS, ROWS, ROWS), F32),
            pltpu.VMEM((ROWS, VALUES), BF16),
            pltpu.VMEM((ROWS, WIDTH), BF16),
            pltpu.VMEM((2 * ROWS, WIDTH), BF16),
            pltpu.VMEM((2 * ROWS, SIDE * HALF), BF16),
            pltpu.VMEM((2 * ROWS, WIDTH), F32),
            pltpu.VMEM((ROWS, WIDTH), BF16),
            pltpu.VMEM((ROWS, WIDTH), BF16),
            dma((5,)),
            dma((3,)),
            dma((3,)),
            dma((3,)),
            dma((3,)),
            dma((3, BLOCKS)),
            dma((2,)),
            dma((6,)),
            dma((4,)),
        ],
        compiler_params=pltpu.CompilerParams(
            collective_id=0, has_side_effects=True, vmem_limit_bytes=67043328
        ),
        name="layer",
    )(*vmem_args, *hbm_args)


def segment_ids(positions, bounds):
    return jnp.sum((positions[:, None] >= bounds[None, :]).astype(jnp.int32), axis=1)


def shards(
    tokens,
    lengths,
    attn_gain,
    w_query,
    w_key,
    w_value,
    w_outgate,
    gate_down,
    gate_up,
    gate_bias,
    conv_weight,
    head_gain,
    w_out,
    forward_norm_scale,
    w_gate,
    w_up,
    down_weight,
):
    group_index = lax.axis_index("req")
    slice_index = lax.axis_index("seq")
    request_slots = lengths.shape[1]
    bounds_all = jnp.cumsum(lengths, axis=1)
    group_row = jnp.arange(lengths.shape[0], dtype=jnp.int32) == group_index
    bounds = jnp.sum(jnp.where(group_row[:, None], bounds_all, 0), axis=0)
    positions = slice_index * ROWS - 3 + jnp.arange(ROWS + 3, dtype=jnp.int32)
    segment_ext = jnp.where(positions < 0, -1, segment_ids(positions, bounds))
    segment = segment_ext[3:]
    columns = [segment >= 0]
    columns += [segment_ext[3 - tap : 3 - tap + ROWS] == segment for tap in (1, 2, 3)]
    columns += [segment == segment[-1], segment == segment_ext[2], segment < request_slots]
    masks = jnp.stack(columns, axis=1).astype(F32)
    masks = jnp.pad(masks, ((0, 0), (0, 128 - masks.shape[1])))
    order = jnp.arange(ROWS)
    allowed = (segment[:, None] == segment[None, :]) & (order[:, None] >= order[None, :])
    padded = [
        jnp.pad(shard, ((0, 0), (0, 2 * HALF - shard.shape[1])))
        for shard in (w_gate, w_up, down_weight)
    ]
    output = layer(
        (
            tokens[0],
            attn_gain[None],
            gate_down,
            gate_up,
            gate_bias[None],
            conv_weight,
            head_gain[None],
            forward_norm_scale[None],
            masks,
            allowed.astype(F32),
        ),
        (w_query, w_key, w_value, w_outgate, w_out, *padded),
    )
    return output[None]


def solution(mesh):
    return jax.shard_map(
        shards,
        mesh=mesh,
        in_specs=(P("req", "seq", None),) + (P(),) * 13 + (P("seq", "req"),) * 3,
        out_specs=P("req", "seq", None),
        check_vma=False,
    )
```

time: 257 us -> 124 us (0.48)
  other arithmetic: 65.2 us -> 3.16 us
  matrix products: 48.7 us -> 0 us
  Pallas kernels: 79.4 us -> 107 us
  blocking collectives: 23.9 us -> 0 us
  starting transfers between devices: 15.9 us -> 0 us
  waiting for transfers between devices: 7.35 us -> 0 us
    dot_general x18 -> x0, matrix products: 48.7 us -> none  [the longest x4 22.2 us: shards(): lax.dot_general(hidden, down_all[quarter], (((1,), (1,)), ((), ())), pref...]
    unnamed x30 -> x0, other arithmetic: 39.6 us -> none
    pallas_call x1, Pallas kernels: 79.4 us -> 107 us  [layer(): pl.pallas_call(layer_kernel, out_shape=jax.ShapeDtypeStruct((ROWS, WIDTH)...]
    all_gather x1 -> x0, blocking collectives: 23.9 us -> none  [shards(): decays = lax.all_gather(decay, 'seq').reshape(devices, devices, piece)]
    reduce_sum x3 -> x0, other arithmetic: 13.7 us -> none  [the longest x1 12.3 us: shards(): jnp.sum(products.reshape(block_rows, block_rows, HEADS, key_width), axis=-1)]
    all_to_all x2 -> x0, starting transfers between devices: 9.15 us -> none  [the longest x1 5.29 us: shards(): lax.all_to_all(pieces, 'seq', split_axis=0, concat_axis=0, tiled=True)]
    ppermute x3 -> x0, starting transfers between devices: 6.75 us -> none  [the longest x1 4.93 us: from_behind(): lax.ppermute(value, axis, [(source, source + steps) for source in range(c...]
    all_to_all x2 -> x0, waiting for transfers between devices: 5.8 us -> none  [the longest x1 5.8 us: shards(): lax.all_to_all(pieces, 'seq', split_axis=0, concat_axis=0, tiled=True)]
  transfers between devices with their start and end apart: 5 -> 0, of which waited for: 2 -> 0; matrix products, arithmetic and copies ran while one was open for 11% -> 0% of each run, Pallas kernels for 31% -> 0%
where the time goes in v2:
time: 124 us; the launch traced here: 123 us
  Pallas kernels  107 us (86%)
  local copies, waits for them, and re-layouts  13.1 us (11%)
  other arithmetic  3.16 us (3%)
    pallas_call x1, Pallas kernels, layer(): pl.pallas_call(layer_kernel, out_shape=jax.ShapeDtypeStruct((ROWS, WIDTH)...  107 us
    pad x3, local copies, waits for them, and re-layouts, shards(): jnp.pad(shard, ((0, 0), (0, 2 * HALF - shard.shape[1])))  4.6 us
    unnamed x2, local copies, waits for them, and re-layouts  3.72 us

profile of v2, /device:TPU:1, one launch (start us, length us, event | category | flops | bytes accessed | tf_op | source)
XLA Modules:
  0.0 123.1 jit_solution(1913202596149864310)
XLA Ops:
  0.0 0.9 reduce_window_sum.11
  0.9 0.1 select_reduce_fusion
  1.0 0.1 convert_reduce_fusion
  1.1 0.1 slice.19
  1.1 0.7 fusion.2
  1.8 1.4 %compare_bitcast_fusion = (pred[128,1]{0,1:T(4,128)(4,1)S(1)}, pred[128,1]{0,1:T(4,128)(4,1)S(1)}, pred[128,1]{0,1:T(4,128)(4,1)S(1)}, pred[128,1]{0,1:T(4,128)(...) fusion(s32[131]{0:T(256)S(1)} %compare_select_fusion, s32[]{:T(128)} %bitcast.6, ...), kind=kLoop, calls=%fused_computation.6 | loop fusion | flops 896 | bytes 2952 | tf_op jit(solution)/shard_map/stack | solution.py:631
  3.2 1.3 %broadcast_in_dim.40.head_gain = bf16[1,512]{1,0:T(2,128)(2,1)} reshape(bf16[512]{0:T(512)(128)(2,1)} %param.28) | data formatting | bytes 2048 | tf_op jit(solution)/shard_map/broadcast_in_dim | solution.py:647
  4.5 1.3 %broadcast_in_dim.38.attn_gain = bf16[1,2048]{1,0:T(2,128)(2,1)} reshape(bf16[2048]{0:T(1024)(128)(2,1)} %param.19) | data formatting | bytes 8192 | tf_op jit(solution)/shard_map/broadcast_in_dim | solution.py:642
  5.8 1.3 %broadcast_in_dim.41.forward_scale = bf16[1,2048]{1,0:T(2,128)(2,1)} reshape(bf16[2048]{0:T(1024)(128)(2,1)} %param.30) | data formatting | bytes 8192 | tf_op jit(solution)/shard_map/broadcast_in_dim | solution.py:648
  7.1 0.1 copy.28
  7.2 1.5 %pad.18.gate_shard = bf16[64,768]{1,0:T(8,128)(2,1)} pad(bf16[64,704]{1,0:T(8,128)(2,1)} %param.31, bf16[]{:T(256)} %constant.29.clone.1), padding=0_0x0_64 | pad | bytes 188418 | tf_op jit(solution)/shard_map/jit(_pad)/pad | solution.py:636
  8.8 1.5 %pad.19.up_shard = bf16[64,768]{1,0:T(8,128)(2,1)} pad(bf16[64,704]{1,0:T(8,128)(2,1)} %param.32, bf16[]{:T(256)} %constant.29.clone.1), padding=0_0x0_64 | pad | bytes 188418 | tf_op jit(solution)/shard_map/jit(_pad)/pad | solution.py:636
  10.3 1.5 %pad.20.down_shard = bf16[64,768]{1,0:T(8,128)(2,1)} pad(bf16[64,704]{1,0:T(8,128)(2,1)} %param.33, bf16[]{:T(256)} %constant.29.clone.1), padding=0_0x0_64 | pad | bytes 188418 | tf_op jit(solution)/shard_map/jit(_pad)/pad | solution.py:636
  11.8 0.7 fusion.1
  12.5 1.8 %copy.29.gate_down = bf16[2048,16]{1,0:T(8,128)(2,1)} copy(bf16[2048,16]{0,1:T(8,128)(2,1)} %param.24) | data formatting | bytes 131072 | tf_op args[7]
  14.4 106.8 %layer.1 = bf16[128,2048]{1,0:T(8,128)(2,1)} custom-call(bf16[128,2048]{1,0:T(8,128)(2,1)} %bitcast.20, bf16[1,2048]{1,0:T(2,128)(2,1)} %broadcast_in_dim.38.attn_gain, bf16[2048,16]{1,0:T(8,128)(2,1)} %copy.29.gate_down, bf16[16,512]{1,0:T(8,128)(2,1)} %gate_up.1, f32[1,512]{1,0:T(1,128)} %bitcast.21, bf16[4,2048]{1,0:T(4,128)(2,1)} %conv_weight.1, ...), custom_call_target="tpu_custom_call" | custom-call | tf_op jit(solution)/shard_map/layer/pallas_call | solution.py:546
  121.2 1.9 %copy.31 = bf16[1,128,2048]{2,1,0:T(8,128)(2,1)} copy(bf16[1,128,2048]{2,1,0:T(8,128)(2,1)} %bitcast.19) | data formatting | bytes 1048576
  (4 shorter events, 0.1 us)

commit v3 on v2

--- a/solution.py
+++ b/solution.py
@@ -16,7 +16,9 @@
 SIDE = 4
 BLOCKS = SIDE**3
 DEVICES = 2 * SIDE * SIDE
-HALF = 384
+HALF = 352
+WIDE = 384
+QUARTER = 2 * HALF
 ROWS = 128
 SUB = 16
 HALO = 16
@@ -26,8 +28,9 @@
 KW = KEYS // HEADS
 VW = VALUES // HEADS
 PIECE = KEYS // DEVICES
+REQUESTS = 4
+VMEM_LIMIT = 56 * 2**20
 ORDERS = (("x", "y", "z"), ("z", "x", "y"), ("y", "z", "x"))
-KEEP, CLEAN, VALID = 4, 5, 6
 
 
 def place():
@@ -68,29 +71,26 @@
 
 
 def layer_kernel(
+    lengths,
     tokens,
-    attn_gain,
+    vectors,
     gate_down,
     gate_up,
-    gate_bias,
     conv_weight,
-    head_gain,
-    forward_scale,
-    masks,
-    allowed,
+    gate_shard,
+    up_shard,
+    down_shard,
     w_query,
     w_key,
     w_value,
     w_outgate,
     w_out_hbm,
-    gate_shard,
-    up_shard,
-    down_shard,
     out,
     wg,
     wu,
     wd,
-    staged,
+    turned,
+    pair_in,
     w_attn,
     w_out,
     normed,
@@ -115,7 +115,6 @@
     other_send,
     other_recv,
     load_sem,
-    local_sem,
     pair_send,
     pair_recv,
     send_sem,
@@ -123,6 +122,7 @@
     halo_sem,
     state_sem,
     swap_sem,
+    out_sem,
 ):
     me = place()
     core = me["c"]
@@ -161,30 +161,32 @@
         pl.semaphore_signal(
             barrier, inc=1, device_id=device_at(moved(me, "y", by)), device_id_type=MESH
         )
+    for part, shard in enumerate((gate_shard, up_shard, down_shard)):
+        columns = jnp.transpose(shard[...].astype(F32))
+        zeros = jnp.zeros_like(columns)
+        turned[part] = jnp.where(
+            core == 0,
+            jnp.concatenate([columns, zeros], axis=1),
+            jnp.concatenate([zeros, columns], axis=1),
+        ).astype(BF16)
+    for quarter in range(SIDE):
+        wd[:, quarter * WIDE + HALF : (quarter + 1) * WIDE, :] = jnp.zeros(
+            (SIDE * SIDE, WIDE - HALF, 128), BF16
+        )
     pl.semaphore_wait(barrier, DEVICES + 1)
 
+    fulls = (wg, wu, wd)
+    strides = (HALF, HALF, WIDE)
+
     def slot(part, at):
-        column = at["x"] * SIDE + at["z"]
-        if part == 2:
-            return wd.at[
-                pl.ds(pl.multiple_of(at["y"] * HALF, 128), HALF),
-                pl.ds(pl.multiple_of(column * 128, 128), 128),
-            ]
-        block = at["y"] * (SIDE * SIDE) + column
-        return (wg, wu)[part].at[pl.ds(pl.multiple_of(block * 128, 128), 128), :]
-
-    def own_half(part, source_core):
-        if part == 2:
-            return staged.at[pl.ds(pl.multiple_of(source_core * 64, 64), 64), :]
-        block = (me["y"] * SIDE + me["x"]) * SIDE + me["z"]
-        first = pl.multiple_of(block * 128 + source_core * 64, 64)
-        return (wg, wu)[part].at[pl.ds(first, 64), :]
-
-    locals_, pairs = [], []
-    for part, shard in enumerate((gate_shard, up_shard, down_shard)):
+        first = pl.multiple_of(at["y"] * strides[part], 32)
+        return fulls[part].at[at["x"] * SIDE + at["z"], pl.ds(first, HALF), :]
+
+    pairs = []
+    for part in range(3):
         pair = pltpu.make_async_remote_copy(
-            src_ref=shard.at[:, pl.ds(pl.multiple_of((1 - core) * HALF, 128), HALF)],
-            dst_ref=own_half(part, core),
+            src_ref=turned.at[part, pl.ds(pl.multiple_of((1 - core) * HALF, 32), HALF), :],
+            dst_ref=pair_in.at[part],
             send_sem=pair_send.at[part],
             recv_sem=pair_recv.at[part],
             device_id=device_at(sibling),
@@ -192,13 +194,6 @@
         )
         pair.start()
         pairs.append(pair)
-        own = pltpu.make_async_copy(
-            shard.at[:, pl.ds(pl.multiple_of(core * HALF, 128), HALF)],
-            own_half(part, core),
-            local_sem.at[part],
-        )
-        own.start()
-        locals_.append(own)
 
     def block_of(at):
         return (at["y"] * SIDE + at["x"]) * SIDE + at["z"]
@@ -240,10 +235,14 @@
             both(part, at, ORDERS[part][1])
             both(part, at, ORDERS[part][2])
 
+    def offset(step):
+        side = jnp.where(step == 1, -onward, onward)
+        return jnp.where(step == 0, 0, jnp.where(step == 3, 2, side))
+
     def second_axis(kind):
         def step_(step, carry):
             for part in range(3):
-                at = at_of(part, step, kinds[kind])
+                at = at_of(part, offset(step), kinds[kind])
                 arrive(part, at)
                 if kind == 0:
                     send(part, at, ORDERS[part][1], onward)
@@ -255,7 +254,7 @@
     def third_axis(kind, second, parts=(0, 1, 2)):
         def step_(step, carry):
             for part in parts:
-                at = at_of(part, step, second, kinds[kind])
+                at = at_of(part, offset(step), second, kinds[kind])
                 arrive(part, at)
                 if kind == 0:
                     send(part, at, ORDERS[part][2], onward)
@@ -266,15 +265,14 @@
     inputs = tokens[...].astype(F32)
     mean_square = jnp.mean(inputs * inputs, axis=-1, keepdims=True)
     normed[...] = (
-        inputs * lax.rsqrt(mean_square + EPSILON) * attn_gain[...].astype(F32)
+        inputs * lax.rsqrt(mean_square + EPSILON) * vectors[0:1, :]
     ).astype(BF16)
 
     for part in range(3):
-        locals_[part].wait()
         pairs[part].wait_recv()
-        if part == 2:
-            ref = slot(2, me)
-            ref[...] = jnp.transpose(staged[...].astype(F32)).astype(BF16)
+        own = turned[part, pl.ds(pl.multiple_of(core * HALF, 32), HALF), :]
+        block = slot(part, me)
+        block[...] = own + pair_in[part]
         both(part, me, ORDERS[part][0])
     for part in range(3):
         both(part, me, ORDERS[part][1])
@@ -312,10 +310,10 @@
 
     loads[3].wait()
     lax.fori_loop(0, 4, project_gate, 0)
-    latent = dot(normed[...], gate_down[...])
+    latent = dot_nt(normed[...], gate_down[...])
     logits = (
         jnp.dot(latent, gate_up[...].astype(F32), precision=HIGHEST, preferred_element_type=F32)
-        + gate_bias[...]
+        + vectors[2:3, 0:KEYS]
     )
     log_decay = (jnp.minimum(logits, 0.0) - jnp.log1p(jnp.exp(-jnp.abs(logits)))) / NORMALIZER
     row = lax.broadcasted_iota(jnp.int32, (ROWS, ROWS), 0)
@@ -323,8 +321,28 @@
     lower = (row >= lane).astype(F32)
     cumulative = jnp.dot(lower, log_decay, precision=HIGHEST, preferred_element_type=F32)
     total[...] = cumulative.reshape(ROWS // SUB, SUB, KEYS)
-    table = masks[...]
-    clean_block = table[ROWS - 1 : ROWS, CLEAN : CLEAN + 1]
+    bounds = [lengths[req, 0]]
+    for slot_index in range(1, REQUESTS):
+        bounds.append(bounds[-1] + lengths[req, slot_index])
+
+    def segment_of(position):
+        count = jnp.zeros_like(position)
+        for bound in bounds:
+            count = count + (position >= bound).astype(jnp.int32)
+        return jnp.where(position < 0, -1, count)
+
+    def column_mask(same):
+        return same.astype(F32)[:, :1]
+
+    position = seq * ROWS + row
+    segment = segment_of(position)
+    allowed = ((segment == segment_of(seq * ROWS + lane)) & (row >= lane)).astype(F32)
+    taps_same = [None] + [column_mask(segment_of(position - tap) == segment) for tap in (1, 2, 3)]
+    last_segment = segment_of(jnp.zeros_like(row) + (seq * ROWS + ROWS - 1))
+    keep = column_mask(segment == last_segment)
+    clean = column_mask(segment == segment_of(jnp.zeros_like(row) + (seq * ROWS - 1)))
+    valid = column_mask(segment < REQUESTS)
+    clean_block = clean[ROWS - 1 : ROWS]
     tail_rows = jnp.dot(
         jnp.transpose(log_decay), jnp.ones((ROWS, 128), F32), precision=HIGHEST,
         preferred_element_type=F32,
@@ -339,8 +357,7 @@
         mixed = rows[HALO:] * taps[0:1]
         for tap in range(1, 4):
             shifted = pltpu.roll(rows, tap, 0)[HALO:]
-            same = table[:, tap : tap + 1]
-            mixed = mixed + taps[tap : tap + 1] * jnp.where(same > 0.0, shifted, 0.0)
+            mixed = mixed + taps[tap : tap + 1] * jnp.where(taps_same[tap] > 0.0, shifted, 0.0)
         mixed = silu(mixed).astype(BF16)
         if chunk == 0:
             query[...] = mixed.astype(F32).reshape(ROWS // SUB, SUB, KEYS)
@@ -351,7 +368,7 @@
 
     tail = cumulative[ROWS - 1 : ROWS]
     keys_left = (
-        keys[...].reshape(ROWS, KEYS) * jnp.exp(tail - cumulative) * table[:, KEEP : KEEP + 1]
+        keys[...].reshape(ROWS, KEYS) * jnp.exp(tail - cumulative) * keep
     )
     for head in range(HEADS):
         high, low = split(jnp.transpose(keys_left[:, head * KW : (head + 1) * KW]))
@@ -446,19 +463,19 @@
 
     exchanged(before, incoming, 2).wait_recv()
     query_decayed = (
-        query[...].reshape(ROWS, KEYS) * jnp.exp(cumulative) * table[:, CLEAN : CLEAN + 1]
+        query[...].reshape(ROWS, KEYS) * jnp.exp(cumulative) * clean
     )
     for head in range(HEADS):
         key_part = slice(head * KW, (head + 1) * KW)
         value_part = slice(head * VW, (head + 1) * VW)
         high, low = split(query_decayed[:, key_part])
-        weights = (scores[head] * allowed[...]).astype(BF16)
+        weights = (scores[head] * allowed).astype(BF16)
         before_state = incoming[key_part, :]
         attended = (
             dot(weights, values[:, value_part]) + dot(high, before_state) + dot(low, before_state)
         )
         mean_square = jnp.mean(attended * attended, axis=-1, keepdims=True)
-        scaled = attended * lax.rsqrt(mean_square + EPSILON) * head_gain[...].astype(F32)
+        scaled = attended * lax.rsqrt(mean_square + EPSILON) * vectors[3:4, 0:VW]
         gated[:, value_part] = (scaled * silu(outgate[:, value_part])).astype(BF16)
 
     load_out.wait()
@@ -475,12 +492,12 @@
     mean_square = jnp.mean(wide * wide, axis=-1, keepdims=True)
     own_rows = pl.ds(pl.multiple_of(core * ROWS, ROWS), ROWS)
     other_rows = pl.ds(pl.multiple_of((1 - core) * ROWS, ROWS), ROWS)
-    x_rows[own_rows, :] = (
-        wide * lax.rsqrt(mean_square + EPSILON) * forward_scale[...].astype(F32)
+    x_rows[:, own_rows] = jnp.transpose(
+        wide * lax.rsqrt(mean_square + EPSILON) * vectors[1:2, :]
     ).astype(BF16)
     swap_x = pltpu.make_async_remote_copy(
-        src_ref=x_rows.at[own_rows, :],
-        dst_ref=x_rows.at[own_rows, :],
+        src_ref=x_rows.at[:, own_rows],
+        dst_ref=x_rows.at[:, own_rows],
         send_sem=swap_sem.at[0],
         recv_sem=swap_sem.at[1],
         device_id=device_at(sibling),
@@ -488,47 +505,74 @@
     )
     swap_x.start()
 
+    def swiglu(quarter):
+        rows = pl.ds(pl.multiple_of(quarter * HALF, 32), HALF)
+
+        def product(full):
+            summed = None
+            for index in range(WIDTH // 256):
+                pair = jnp.concatenate([full[2 * index, rows, :], full[2 * index + 1, rows, :]], axis=1)
+                term = dot(pair, x_rows[index * 256 : (index + 1) * 256, :])
+                summed = term if summed is None else summed + term
+            return summed
+
+        units = silu(product(wg)) * product(wu)
+        units = jnp.concatenate([units, jnp.zeros((WIDE - HALF, 2 * ROWS), F32)], axis=0)
+        columns = pl.ds(pl.multiple_of(quarter * WIDE, 128), WIDE)
+        hidden[:, columns] = jnp.transpose(units).astype(BF16)
+
     for second in kinds:
         third_axis(0, second)
-    for second in (0,) + kinds:
+    third_axis(1, 0)
+    for second in kinds:
         third_axis(1, second)
-        third_axis(2, second)
     swap_x.wait()
-
-    for quarter in range(SIDE):
-        columns = slice(quarter * HALF, (quarter + 1) * HALF)
-        features = slice(quarter * WIDTH, (quarter + 1) * WIDTH)
-        gate = dot(x_rows[...], wg[features, :])
-        upward = dot(x_rows[...], wu[features, :])
-        hidden[:, columns] = (silu(gate) * upward).astype(BF16)
+    third_axis(2, 0, (0, 2))
+    swiglu(me["y"])
+    for order, second in enumerate(kinds):
+        third_axis(2, second, (0, 2))
+        if order == 2:
+            for step in (0,) + kinds:
+                third_axis(2, step, (1,))
+        swiglu((me["y"] + second + SIDE) % SIDE)
+
+    def swap_out(index):
+        columns = pl.ds(pl.multiple_of(index * 256, 256), 256)
+        return pltpu.make_async_remote_copy(
+            src_ref=other_send.at[:, columns],
+            dst_ref=other_recv.at[:, columns],
+            send_sem=out_sem.at[0, index],
+            recv_sem=out_sem.at[1, index],
+            device_id=device_at(sibling),
+            device_id_type=MESH,
+        )
 
     def project_down(index, carry):
         columns = pl.ds(pl.multiple_of(index * 256, 256), 256)
-        acc[:, columns] = dot(hidden[...], wd[:, columns])
+        pair = jnp.concatenate([wd[2 * index], wd[2 * index + 1]], axis=1)
+        acc[:, columns] = dot(hidden[...], pair)
+        other_send[:, columns] = acc[other_rows, columns].astype(BF16)
+        swap_out(index).start()
         return carry
 
     lax.fori_loop(0, WIDTH // 256, project_down, 0)
-    other_send[...] = acc[other_rows, :].astype(BF16)
-    swap_out = pltpu.make_async_remote_copy(
-        src_ref=other_send,
-        dst_ref=other_recv,
-        send_sem=swap_sem.at[2],
-        recv_sem=swap_sem.at[3],
-        device_id=device_at(sibling),
-        device_id_type=MESH,
-    )
-    swap_out.start()
-    swap_out.wait()
-    mlp = (acc[own_rows, :] + other_recv[...].astype(F32)).astype(BF16)
-    result = resident[...].astype(F32) + mlp.astype(F32)
-    out[...] = jnp.where(table[:, VALID : VALID + 1] > 0.0, result, 0.0).astype(BF16)
+
+    def finish(index, carry):
+        columns = pl.ds(pl.multiple_of(index * 256, 256), 256)
+        swap_out(index).wait()
+        mlp = (acc[own_rows, columns] + other_recv[:, columns].astype(F32)).astype(BF16)
+        result = resident[:, columns].astype(F32) + mlp.astype(F32)
+        out[:, columns] = jnp.where(valid > 0.0, result, 0.0).astype(BF16)
+        return carry
+
+    lax.fori_loop(0, WIDTH // 256, finish, 0)
 
     exchanged(decay_out, decay_in, 0).wait_send()
     exchanged(state_out, state_in, 1).wait_send()
     exchanged(before, incoming, 2).wait_send()
     for part in range(3):
         pairs[part].wait_send()
-        sent = wg.at[pl.ds(0, (BLOCKS - 1) * 128), :]
+        sent = w_attn.at[pl.ds(0, 66 * 16), pl.ds(0, 21 * 128)]
         pltpu.make_async_remote_copy(
             src_ref=sent,
             dst_ref=sent,
@@ -539,20 +583,23 @@
         ).wait_send()
 
 
-def layer(vmem_args, hbm_args):
+def layer(lengths, vmem_args, hbm_args):
     vmem = pl.BlockSpec(memory_space=pltpu.VMEM)
-    hbm = pl.BlockSpec(memory_space=pl.ANY)
+    hbm = pl.BlockSpec(memory_space=pltpu.HBM)
     dma = pltpu.SemaphoreType.DMA
     return pl.pallas_call(
         layer_kernel,
         out_shape=jax.ShapeDtypeStruct((ROWS, WIDTH), BF16),
-        in_specs=[vmem] * len(vmem_args) + [hbm] * len(hbm_args),
+        in_specs=[pl.BlockSpec(memory_space=pltpu.SMEM)]
+        + [vmem] * len(vmem_args)
+        + [hbm] * len(hbm_args),
         out_specs=vmem,
         scratch_shapes=[
-            pltpu.VMEM((BLOCKS * 128, HALF), BF16),
-            pltpu.VMEM((BLOCKS * 128, HALF), BF16),
-            pltpu.VMEM((SIDE * HALF, WIDTH), BF16),
-            pltpu.VMEM((128, HALF), BF16),
+            pltpu.VMEM((SIDE * SIDE, SIDE * HALF, 128), BF16),
+            pltpu.VMEM((SIDE * SIDE, SIDE * HALF, 128), BF16),
+            pltpu.VMEM((SIDE * SIDE, SIDE * WIDE, 128), BF16),
+            pltpu.VMEM((3, QUARTER, 128), BF16),
+            pltpu.VMEM((3, HALF, 128), BF16),
             pltpu.VMEM((WIDTH, 2 * KEYS + 2 * VALUES), BF16),
             pltpu.VMEM((VALUES, WIDTH), BF16),
             pltpu.VMEM((ROWS, WIDTH), BF16),
@@ -571,8 +618,8 @@
             pltpu.VMEM((HEADS, ROWS, ROWS), F32),
             pltpu.VMEM((ROWS, VALUES), BF16),
             pltpu.VMEM((ROWS, WIDTH), BF16),
-            pltpu.VMEM((2 * ROWS, WIDTH), BF16),
-            pltpu.VMEM((2 * ROWS, SIDE * HALF), BF16),
+            pltpu.VMEM((WIDTH, 2 * ROWS), BF16),
+            pltpu.VMEM((2 * ROWS, SIDE * WIDE), BF16),
             pltpu.VMEM((2 * ROWS, WIDTH), F32),
             pltpu.VMEM((ROWS, WIDTH), BF16),
             pltpu.VMEM((ROWS, WIDTH), BF16),
@@ -580,21 +627,17 @@
             dma((3,)),
             dma((3,)),
             dma((3,)),
-            dma((3,)),
             dma((3, BLOCKS)),
             dma((2,)),
             dma((6,)),
-            dma((4,)),
+            dma((2,)),
+            dma((2, WIDTH // 256)),
         ],
         compiler_params=pltpu.CompilerParams(
-            collective_id=0, has_side_effects=True, vmem_limit_bytes=67043328
+            collective_id=0, has_side_effects=True, vmem_limit_bytes=VMEM_LIMIT
         ),
         name="layer",
-    )(*vmem_args, *hbm_args)
-
-
-def segment_ids(positions, bounds):
-    return jnp.sum((positions[:, None] >= bounds[None, :]).astype(jnp.int32), axis=1)
+    )(lengths, *vmem_args, *hbm_args)
 
 
 def shards(
@@ -616,40 +659,21 @@
     w_up,
     down_weight,
 ):
-    group_index = lax.axis_index("req")
-    slice_index = lax.axis_index("seq")
-    request_slots = lengths.shape[1]
-    bounds_all = jnp.cumsum(lengths, axis=1)
-    group_row = jnp.arange(lengths.shape[0], dtype=jnp.int32) == group_index
-    bounds = jnp.sum(jnp.where(group_row[:, None], bounds_all, 0), axis=0)
-    positions = slice_index * ROWS - 3 + jnp.arange(ROWS + 3, dtype=jnp.int32)
-    segment_ext = jnp.where(positions < 0, -1, segment_ids(positions, bounds))
-    segment = segment_ext[3:]
-    columns = [segment >= 0]
-    columns += [segment_ext[3 - tap : 3 - tap + ROWS] == segment for tap in (1, 2, 3)]
-    columns += [segment == segment[-1], segment == segment_ext[2], segment < request_slots]
-    masks = jnp.stack(columns, axis=1).astype(F32)
-    masks = jnp.pad(masks, ((0, 0), (0, 128 - masks.shape[1])))
-    order = jnp.arange(ROWS)
-    allowed = (segment[:, None] == segment[None, :]) & (order[:, None] >= order[None, :])
-    padded = [
-        jnp.pad(shard, ((0, 0), (0, 2 * HALF - shard.shape[1])))
-        for shard in (w_gate, w_up, down_weight)
-    ]
+    rows = [attn_gain, forward_norm_scale, gate_bias, head_gain]
+    vectors = jnp.stack([jnp.pad(row.astype(F32), (0, WIDTH - row.shape[0])) for row in rows])
     output = layer(
+        lengths,
         (
             tokens[0],
-            attn_gain[None],
-            gate_down,
+            vectors,
+            gate_down.T,
             gate_up,
-            gate_bias[None],
             conv_weight,
-            head_gain[None],
-            forward_norm_scale[None],
-            masks,
-            allowed.astype(F32),
+            w_gate,
+            w_up,
+            down_weight,
         ),
-        (w_query, w_key, w_value, w_outgate, w_out, *padded),
+        (w_query, w_key, w_value, w_outgate, w_out),
     )
     return output[None]
 

time: 124 us -> 102 us (0.82)
  Pallas kernels: 107 us -> 96.1 us
  local copies, waits for them, and re-layouts: 13.1 us -> 2.57 us
    pallas_call x1, Pallas kernels: 107 us -> 96.1 us  [layer(): pl.pallas_call(layer_kernel, out_shape=jax.ShapeDtypeStruct((ROWS, WIDTH)...]
    pad x3 -> x1, local copies, waits for them, and re-layouts: 4.6 us -> 0.68 us  [shards(): jnp.pad(row.astype(F32), (0, WIDTH - row.shape[0]))]
    broadcast_in_dim x3 -> x0, local copies, waits for them, and re-layouts: 3.83 us -> none  [the longest x1 1.29 us: shards(): forward_norm_scale[None]]
    unnamed x2 -> x1, local copies, waits for them, and re-layouts: 3.72 us -> 1.88 us
    another operation x2 -> x4, other arithmetic: 2.26 us -> 2.71 us  [shards(): jnp.stack([jnp.pad(row.astype(F32), (0, WIDTH - row.shape[0])) for row in...]
where the time goes in v3:
time: 102 us; the launch traced here: 101 us
  Pallas kernels  96.1 us (94%)
  other arithmetic  2.71 us (3%)
  local copies, waits for them, and re-layouts  2.57 us (3%)
    pallas_call x1, Pallas kernels, layer(): pl.pallas_call(layer_kernel, out_shape=jax.ShapeDtypeStruct((ROWS, WIDTH)...  96.1 us
    another operation x4, other arithmetic, shards(): jnp.stack([jnp.pad(row.astype(F32), (0, WIDTH - row.shape[0])) for row in...  2.71 us

profile of v3, /device:TPU:1, one launch (start us, length us, event | category | flops | bytes accessed | tf_op | source)
XLA Modules:
  0.0 101.4 jit_solution(11498270359107593925)
XLA Ops:
  0.0 0.7 stack.32
  0.7 0.7 pad.8
  1.4 0.7 pad_convert_fusion
  2.1 0.7 stack.33
  2.7 0.7 pad_maximum_fusion.vectors
  3.4 96.1 %layer.1 = bf16[128,2048]{1,0:T(8,128)(2,1)} custom-call(s32[4,4]{1,0:T(4,128)} %lengths.1, bf16[128,2048]{1,0:T(8,128)(2,1)} %bitcast.8, f32[4,2048]{1,0:T(4,128)} %pad_maximum_fusion.vectors, bf16[16,2048]{1,0:T(8,128)(2,1)} %bitcast.9, bf16[16,512]{1,0:T(8,128)(2,1)} %gate_up.1, bf16[4,2048]{1,0:T(4,128)(2,1)} %conv_weight.1, bf16[64,704]{1,0:T(8,128)(2,1)} %gate_shard.1, ...), custom_call_target="tpu_custom_call" | custom-call | tf_op jit(solution)/shard_map/layer/pallas_call | solution.py:590
  99.5 1.9 %copy.19 = bf16[1,128,2048]{2,1,0:T(8,128)(2,1)} copy(bf16[1,128,2048]{2,1,0:T(8,128)(2,1)} %bitcast.7) | data formatting | bytes 1048576

commit v4 on v3

--- a/solution.py
+++ b/solution.py
@@ -27,7 +27,8 @@
 VALUES = 1024
 KW = KEYS // HEADS
 VW = VALUES // HEADS
-PIECE = KEYS // DEVICES
+CHIPS = SIDE * SIDE
+PIECE = KW // CHIPS
 REQUESTS = 4
 VMEM_LIMIT = 56 * 2**20
 ORDERS = (("x", "y", "z"), ("z", "x", "y"), ("y", "z", "x"))
@@ -72,11 +73,14 @@
 
 def layer_kernel(
     lengths,
-    tokens,
-    vectors,
+    attn_gain,
+    forward_scale,
+    gate_bias,
+    head_gain,
     gate_down,
     gate_up,
     conv_weight,
+    tokens_hbm,
     gate_shard,
     up_shard,
     down_shard,
@@ -86,6 +90,8 @@
     w_outgate,
     w_out_hbm,
     out,
+    tokens,
+    raw,
     wg,
     wu,
     wd,
@@ -100,11 +106,16 @@
     keys,
     values,
     total,
+    state_own,
+    decay_own,
+    state_other,
+    decay_other,
     state_out,
     decay_out,
     state_in,
     decay_in,
     before,
+    chip_incoming,
     incoming,
     scores,
     gated,
@@ -123,6 +134,7 @@
     state_sem,
     swap_sem,
     out_sem,
+    core_sem,
 ):
     me = place()
     core = me["c"]
@@ -131,6 +143,13 @@
     sibling = dict(me, c=1 - core)
     onward = 1 - 2 * core
 
+    shard_loads = []
+    for part, shard in enumerate((gate_shard, up_shard, down_shard)):
+        load = pltpu.make_async_copy(shard, raw.at[part], load_sem.at[6 + part])
+        load.start()
+        shard_loads.append(load)
+    load_tokens = pltpu.make_async_copy(tokens_hbm, tokens, load_sem.at[5])
+    load_tokens.start()
     loads = []
     for index, (source, first, count) in enumerate(
         (
@@ -152,28 +171,29 @@
 
     def greet(step, carry):
         pl.semaphore_signal(
-            barrier, inc=1, device_id=(req, (seq + step) % DEVICES), device_id_type=MESH
+            barrier, inc=1, device_id=(req, (seq + 2 * step) % DEVICES), device_id_type=MESH
         )
         return carry
 
-    lax.fori_loop(1, DEVICES, greet, 0)
+    lax.fori_loop(1, CHIPS, greet, 0)
+    for by in (1, DEVICES - 1):
+        pl.semaphore_signal(
+            barrier, inc=1, device_id=(req, (seq + by) % DEVICES), device_id_type=MESH
+        )
     for by in (1, -1):
         pl.semaphore_signal(
             barrier, inc=1, device_id=device_at(moved(me, "y", by)), device_id_type=MESH
         )
-    for part, shard in enumerate((gate_shard, up_shard, down_shard)):
-        columns = jnp.transpose(shard[...].astype(F32))
+    for part in range(3):
+        shard_loads[part].wait()
+        columns = jnp.transpose(raw[part].astype(F32))
         zeros = jnp.zeros_like(columns)
         turned[part] = jnp.where(
             core == 0,
             jnp.concatenate([columns, zeros], axis=1),
             jnp.concatenate([zeros, columns], axis=1),
         ).astype(BF16)
-    for quarter in range(SIDE):
-        wd[:, quarter * WIDE + HALF : (quarter + 1) * WIDE, :] = jnp.zeros(
-            (SIDE * SIDE, WIDE - HALF, 128), BF16
-        )
-    pl.semaphore_wait(barrier, DEVICES + 1)
+    pl.semaphore_wait(barrier, CHIPS + 3)
 
     fulls = (wg, wu, wd)
     strides = (HALF, HALF, WIDE)
@@ -261,12 +281,6 @@
             return carry
 
         lax.fori_loop(0, SIDE, step_, 0)
-
-    inputs = tokens[...].astype(F32)
-    mean_square = jnp.mean(inputs * inputs, axis=-1, keepdims=True)
-    normed[...] = (
-        inputs * lax.rsqrt(mean_square + EPSILON) * vectors[0:1, :]
-    ).astype(BF16)
 
     for part in range(3):
         pairs[part].wait_recv()
@@ -278,6 +292,18 @@
         both(part, me, ORDERS[part][1])
     for part in range(3):
         both(part, me, ORDERS[part][2])
+
+    load_tokens.wait()
+    inputs = tokens[...].astype(F32)
+    mean_square = jnp.mean(inputs * inputs, axis=-1, keepdims=True)
+    normed[...] = (
+        inputs * lax.rsqrt(mean_square + EPSILON) * attn_gain[...].astype(F32).reshape(1, WIDTH)
+    ).astype(BF16)
+
+    for quarter in range(SIDE):
+        wd[:, quarter * WIDE + HALF : (quarter + 1) * WIDE, :] = jnp.zeros(
+            (SIDE * SIDE, WIDE - HALF, 128), BF16
+        )
 
     def project(index, carry):
         columns = pl.ds(pl.multiple_of(index * 256, 256), 256)
@@ -313,7 +339,7 @@
     latent = dot_nt(normed[...], gate_down[...])
     logits = (
         jnp.dot(latent, gate_up[...].astype(F32), precision=HIGHEST, preferred_element_type=F32)
-        + vectors[2:3, 0:KEYS]
+        + gate_bias[...].reshape(1, KEYS)
     )
     log_decay = (jnp.minimum(logits, 0.0) - jnp.log1p(jnp.exp(-jnp.abs(logits)))) / NORMALIZER
     row = lax.broadcasted_iota(jnp.int32, (ROWS, ROWS), 0)
@@ -347,7 +373,7 @@
         jnp.transpose(log_decay), jnp.ones((ROWS, 128), F32), precision=HIGHEST,
         preferred_element_type=F32,
     )
-    decay_out[...] = jnp.exp(tail_rows) * clean_block
+    decay_own[...] = jnp.exp(tail_rows) * clean_block
 
     halo.wait()
     for chunk in range(4):
@@ -373,19 +399,34 @@
     for head in range(HEADS):
         high, low = split(jnp.transpose(keys_left[:, head * KW : (head + 1) * KW]))
         head_values = values[:, head * VW : (head + 1) * VW]
-        state_out[head * KW : (head + 1) * KW, :] = (
+        state_own[head * KW : (head + 1) * KW, :] = (
             dot(high, head_values) + dot(low, head_values)
         ).astype(BF16)
 
+    def to_sibling(source, target, which):
+        return pltpu.make_async_remote_copy(
+            src_ref=source,
+            dst_ref=target,
+            send_sem=core_sem.at[0, which],
+            recv_sem=core_sem.at[1, which],
+            device_id=device_at(sibling),
+            device_id_type=MESH,
+        )
+
+    swap_state = to_sibling(state_own, state_other, 0)
+    swap_state.start()
+    swap_decay = to_sibling(decay_own, decay_other, 1)
+    swap_decay.start()
+
     def piece_of(ref, index):
         return ref.at[pl.ds(pl.multiple_of(index * PIECE, PIECE), PIECE), :]
 
     def exchange(source, target, which):
         def step_(step, carry):
-            to = (seq + step) % DEVICES
+            to = (seq + 2 * step) % DEVICES
             pltpu.make_async_remote_copy(
-                src_ref=piece_of(source, to),
-                dst_ref=piece_of(target, seq),
+                src_ref=piece_of(source, to // 2),
+                dst_ref=piece_of(target, seq // 2),
                 send_sem=state_sem.at[2 * which],
                 recv_sem=state_sem.at[2 * which + 1],
                 device_id=(req, to),
@@ -393,10 +434,10 @@
             ).start()
             return carry
 
-        lax.fori_loop(1, DEVICES, step_, 0)
+        lax.fori_loop(1, CHIPS, step_, 0)
 
     def exchanged(source, target, which):
-        count = (DEVICES - 1) * PIECE
+        count = (CHIPS - 1) * PIECE
         return pltpu.make_async_remote_copy(
             src_ref=source.at[pl.ds(0, count), :],
             dst_ref=target.at[pl.ds(0, count), :],
@@ -406,9 +447,26 @@
             device_id_type=MESH,
         )
 
+    def wide_decay(decay):
+        return jnp.concatenate([decay] * (VW // 128), axis=1)
+
+    head_rows = pl.ds(pl.multiple_of(core * KW, KW), KW)
+    swap_state.wait_recv()
+    swap_decay.wait_recv()
+    own_state = state_own[head_rows, :].astype(F32)
+    own_decay = decay_own[head_rows, :]
+    other_state = state_other[head_rows, :].astype(F32)
+    other_decay = decay_other[head_rows, :]
+    first = core == 0
+    earlier = jnp.where(first, own_state, other_state)
+    later = jnp.where(first, other_state, own_state)
+    later_decay = jnp.where(first, other_decay, own_decay)
+    state_out[...] = (earlier * wide_decay(later_decay) + later).astype(BF16)
+    decay_out[...] = own_decay * other_decay
+
     exchange(decay_out, decay_in, 0)
     exchange(state_out, state_in, 1)
-    mine = pl.ds(pl.multiple_of(seq * PIECE, PIECE), PIECE)
+    mine = pl.ds(pl.multiple_of((seq // 2) * PIECE, PIECE), PIECE)
     decay_in[mine, :] = decay_out[mine, :]
     state_in[mine, :] = state_out[mine, :]
 
@@ -449,19 +507,28 @@
     def prefix(step, running):
         rows = pl.ds(pl.multiple_of(step * PIECE, PIECE), PIECE)
         before[rows, :] = running.astype(BF16)
-        decay = decay_in[rows, :]
-        decay = jnp.concatenate([decay] * (VW // 128), axis=1)
-        return running * decay + state_in[rows, :].astype(F32)
-
-    lax.fori_loop(0, DEVICES, prefix, jnp.zeros((PIECE, VW), F32))
-    exchange(before, incoming, 2)
-    incoming[mine, :] = before[mine, :]
+        return running * wide_decay(decay_in[rows, :]) + state_in[rows, :].astype(F32)
+
+    lax.fori_loop(0, CHIPS, prefix, jnp.zeros((PIECE, VW), F32))
+    exchange(before, chip_incoming, 2)
+    chip_incoming[mine, :] = before[mine, :]
 
     second_axis(1)
     second_axis(2)
     third_axis(0, 0)
 
-    exchanged(before, incoming, 2).wait_recv()
+    exchanged(before, chip_incoming, 2).wait_recv()
+    incoming[head_rows, :] = chip_incoming[...]
+    swap_incoming = pltpu.make_async_remote_copy(
+        src_ref=chip_incoming,
+        dst_ref=incoming.at[head_rows, :],
+        send_sem=core_sem.at[0, 2],
+        recv_sem=core_sem.at[1, 2],
+        device_id=device_at(sibling),
+        device_id_type=MESH,
+    )
+    swap_incoming.start()
+    swap_incoming.wait()
     query_decayed = (
         query[...].reshape(ROWS, KEYS) * jnp.exp(cumulative) * clean
     )
@@ -471,11 +538,16 @@
         high, low = split(query_decayed[:, key_part])
         weights = (scores[head] * allowed).astype(BF16)
         before_state = incoming[key_part, :]
+        after_first = (
+            before_state.astype(F32) * wide_decay(decay_other[key_part, :])
+            + state_other[key_part, :].astype(F32)
+        ).astype(BF16)
+        before_state = jnp.where(first, before_state, after_first)
         attended = (
             dot(weights, values[:, value_part]) + dot(high, before_state) + dot(low, before_state)
         )
         mean_square = jnp.mean(attended * attended, axis=-1, keepdims=True)
-        scaled = attended * lax.rsqrt(mean_square + EPSILON) * vectors[3:4, 0:VW]
+        scaled = attended * lax.rsqrt(mean_square + EPSILON) * head_gain[...].astype(F32).reshape(1, VW)
         gated[:, value_part] = (scaled * silu(outgate[:, value_part])).astype(BF16)
 
     load_out.wait()
@@ -493,7 +565,7 @@
     own_rows = pl.ds(pl.multiple_of(core * ROWS, ROWS), ROWS)
     other_rows = pl.ds(pl.multiple_of((1 - core) * ROWS, ROWS), ROWS)
     x_rows[:, own_rows] = jnp.transpose(
-        wide * lax.rsqrt(mean_square + EPSILON) * vectors[1:2, :]
+        wide * lax.rsqrt(mean_square + EPSILON) * forward_scale[...].astype(F32).reshape(1, WIDTH)
     ).astype(BF16)
     swap_x = pltpu.make_async_remote_copy(
         src_ref=x_rows.at[:, own_rows],
@@ -569,7 +641,9 @@
 
     exchanged(decay_out, decay_in, 0).wait_send()
     exchanged(state_out, state_in, 1).wait_send()
-    exchanged(before, incoming, 2).wait_send()
+    exchanged(before, chip_incoming, 2).wait_send()
+    swap_state.wait_send()
+    swap_decay.wait_send()
     for part in range(3):
         pairs[part].wait_send()
         sent = w_attn.at[pl.ds(0, 66 * 16), pl.ds(0, 21 * 128)]
@@ -595,6 +669,8 @@
         + [hbm] * len(hbm_args),
         out_specs=vmem,
         scratch_shapes=[
+            pltpu.VMEM((ROWS, WIDTH), BF16),
+            pltpu.VMEM((3, 64, QUARTER), BF16),
             pltpu.VMEM((SIDE * SIDE, SIDE * HALF, 128), BF16),
             pltpu.VMEM((SIDE * SIDE, SIDE * HALF, 128), BF16),
             pltpu.VMEM((SIDE * SIDE, SIDE * WIDE, 128), BF16),
@@ -613,7 +689,12 @@
             pltpu.VMEM((KEYS, 128), F32),
             pltpu.VMEM((KEYS, VW), BF16),
             pltpu.VMEM((KEYS, 128), F32),
-            pltpu.VMEM((KEYS, VW), BF16),
+            pltpu.VMEM((KW, VW), BF16),
+            pltpu.VMEM((KW, 128), F32),
+            pltpu.VMEM((KW, VW), BF16),
+            pltpu.VMEM((KW, 128), F32),
+            pltpu.VMEM((KW, VW), BF16),
+            pltpu.VMEM((KW, VW), BF16),
             pltpu.VMEM((KEYS, VW), BF16),
             pltpu.VMEM((HEADS, ROWS, ROWS), F32),
             pltpu.VMEM((ROWS, VALUES), BF16),
@@ -623,7 +704,7 @@
             pltpu.VMEM((2 * ROWS, WIDTH), F32),
             pltpu.VMEM((ROWS, WIDTH), BF16),
             pltpu.VMEM((ROWS, WIDTH), BF16),
-            dma((5,)),
+            dma((9,)),
             dma((3,)),
             dma((3,)),
             dma((3,)),
@@ -632,6 +713,7 @@
             dma((6,)),
             dma((2,)),
             dma((2, WIDTH // 256)),
+            dma((2, 3)),
         ],
         compiler_params=pltpu.CompilerParams(
             collective_id=0, has_side_effects=True, vmem_limit_bytes=VMEM_LIMIT
@@ -659,21 +741,20 @@
     w_up,
     down_weight,
 ):
-    rows = [attn_gain, forward_norm_scale, gate_bias, head_gain]
-    vectors = jnp.stack([jnp.pad(row.astype(F32), (0, WIDTH - row.shape[0])) for row in rows])
     output = layer(
         lengths,
+        (attn_gain, forward_norm_scale, gate_bias, head_gain, gate_down.T, gate_up, conv_weight),
         (
             tokens[0],
-            vectors,
-            gate_down.T,
-            gate_up,
-            conv_weight,
             w_gate,
             w_up,
             down_weight,
+            w_query,
+            w_key,
+            w_value,
+            w_outgate,
+            w_out,
         ),
-        (w_query, w_key, w_value, w_outgate, w_out),
     )
     return output[None]
 

time: 102 us -> 93.1 us (0.913)
  Pallas kernels: 96.1 us -> 91 us
  other arithmetic: 2.71 us -> 0 us
    pallas_call x1, Pallas kernels: 96.1 us -> 91 us  [layer(): pl.pallas_call(layer_kernel, out_shape=jax.ShapeDtypeStruct((ROWS, WIDTH)...]
    another operation x4 -> x0, other arithmetic: 2.71 us -> none  [shards(): jnp.stack([jnp.pad(row.astype(F32), (0, WIDTH - row.shape[0])) for row in...]
where the time goes in v4:
time: 93.1 us; the launch traced here: 92.9 us
  Pallas kernels  91 us (98%)
  local copies, waits for them, and re-layouts  1.88 us (2%)
    pallas_call x1, Pallas kernels, layer(): pl.pallas_call(layer_kernel, out_shape=jax.ShapeDtypeStruct((ROWS, WIDTH)...  91 us
    unnamed x1, local copies, waits for them, and re-layouts  1.88 us

profile of v4, /device:TPU:1, one launch (start us, length us, event | category | flops | bytes accessed | tf_op | source)
XLA Modules:
  0.0 92.9 jit_solution(7929733114014235021)
XLA Ops:
  0.0 91.0 %layer.1 = bf16[128,2048]{1,0:T(8,128)(2,1)} custom-call(s32[4,4]{1,0:T(4,128)} %lengths.1, bf16[2048]{0:T(1024)(128)(2,1)} %attn_gain.1, bf16[2048]{0:T(1024)(128)(2,1)} %forward_scale.1, f32[512]{0:T(512)} %gate_bias.1, bf16[512]{0:T(512)(128)(2,1)} %head_gain.1, bf16[16,2048]{1,0:T(8,128)(2,1)} %bitcast.5, bf16[16,512]{1,0:T(8,128)(2,1)} %gate_up.1, ...), custom_call_target="tpu_custom_call" | custom-call | tf_op jit(solution)/shard_map/layer/pallas_call | solution.py:664
  91.0 1.9 %copy.19 = bf16[1,128,2048]{2,1,0:T(8,128)(2,1)} copy(bf16[1,128,2048]{2,1,0:T(8,128)(2,1)} %bitcast.3) | data formatting | bytes 1048576
